TPU v7x, 128 devices: a whole 4x4x4 slice. The times are simulated.
128 devices in a mesh: gx: 8 (over z, core), gy: 16 (over y, x).
Axes of the slice: x: 4, y: 4, z: 4, core: 2. Of those that a mesh axis runs over, the one named last changes fastest.
Arguments:
- water_depth: float32 [512, 4096], P('gx', 'gy'), may hold values from 0.2 to 4
- bed_level: float32 [512, 4096], P('gx', 'gy'), may hold values from -1.2 to 1.2
- roughness: float32 [512, 4096], P('gx', 'gy'), may hold values from 0.03 to 0.15
- wet_mask: int32 [512, 4096], P('gx', 'gy'), may hold values 0 or 1
- flux_east: float32 [512, 4096], P('gx', 'gy'), may hold values from -3 to 3
- flux_south: float32 [512, 4096], P('gx', 'gy'), may hold values from -3 to 3
- bank_row: int32 [4194304], P(('gx', 'gy')), may hold values from 0 to 63
- bank_column: int32 [4194304], P(('gx', 'gy')), may hold values from 0 to 255
- link_section: int32 [4194304], P(('gx', 'gy')), may hold values from 0 to 31
- link_reach: int32 [4194304], P(('gx', 'gy')), may hold values from 0 to 511
- link_crest: float32 [4194304], P(('gx', 'gy')), may hold values from 0.5 to 3
- link_factor: float32 [4194304], P(('gx', 'gy')), may hold values from 0.2 to 1
- link_regime: int32 [4194304], P(('gx', 'gy')), may hold values from 0 to 2
- channel_segment: float32 [4096, 512], P(('gx', 'gy')), may hold values from -1 to 5.2
- old_discharge: float32 [4096, 512], P(('gx', 'gy')), may hold values from -6 to 6
- courant: float32 [4096, 512], P(('gx', 'gy')), may hold values from 30 to 6144000
- junction: int32 [4096, 512], P(('gx', 'gy')), may hold values 0 or 1
- pass_share: float32 [4096, 512], P(('gx', 'gy')), may hold values from 0.5 to 0.8
- inflow: float32 [512], replicated, may hold values from -5 to 5
Outputs:
- new_depth: float32 [512, 4096], P('gx', 'gy')
- new_flux_east: float32 [512, 4096], P('gx', 'gy')
- new_flux_south: float32 [512, 4096], P('gx', 'gy')
- new_discharge: float32 [4096, 512], P(('gx', 'gy'))
All inputs are finite; a program needn't handle non-finite values. No bound on the sum of `wet_mask` or of `junction` on one device may be relied on, other than what follows from the above.
Results may differ from a plain program's by a relative error of at most 0.00029.
Values sent between devices are 32-bit elements; how exact they have to be, the bound alone decides.
A program may use at most 64 MiB of HBM per device.

v0:
```python
import jax
import jax.numpy as jnp
from jax import lax
from jax.sharding import PartitionSpec as P

SUBSTEPS = 4


GRAVITY = 9.81
SPACING = 20.0
TIME_STEP = 2.2
MIN_FLOW_DEPTH = 0.3
IMPLICIT_WEIGHT = 0.6
LATERAL_SCALE = 0.01
BANK_GAIN = 0.5


def with_halo(shard, sides, width):
    for axis, dim in sides:
        size, length = (lax.axis_size(axis), shard.shape[dim])
        up = [(i, (i + 1) % size) for i in range(size - 1)]
        down = [(j, i) for i, j in up]
        last = lax.slice_in_dim(shard, length - width, length, axis=dim)
        first = lax.slice_in_dim(shard, 0, width, axis=dim)
        before = lax.ppermute(last, axis, up)
        after = lax.ppermute(first, axis, down)
        shard = jnp.concatenate([before, shard, after], axis=dim)
    return shard


def entering(part, axis, combine, identity):
    place = lax.axis_index(axis)
    gathered = jax.tree.map(lambda a: lax.all_gather(a, axis), part)
    state = jax.tree.map(lambda a, e: jnp.zeros_like(a) + jnp.asarray(e, a.dtype), part, identity)

    def one(step, state):
        return combine(
            state, jax.tree.map(lambda a: lax.dynamic_index_in_dim(a, step, 0, False), gathered)
        )

    return lax.fori_loop(0, place, one, state)


def face_update(
    surface_near, surface_far, bed_near, bed_far, rough_near, rough_far, wet_near, wet_far, flux_old
):
    flow_depth = jnp.maximum(
        jnp.maximum(surface_near, surface_far) - jnp.maximum(bed_near, bed_far), MIN_FLOW_DEPTH
    )
    manning = 0.5 * (rough_near + rough_far)
    slope = (surface_far - surface_near) / SPACING
    friction = 1.0 + GRAVITY * TIME_STEP * manning * manning * jnp.abs(flux_old) / jnp.power(
        flow_depth, 7.0 / 3.0
    )
    return wet_near * wet_far * (flux_old - GRAVITY * TIME_STEP * flow_depth * slope) / friction


def substep(water, east, south, bed, rough, wetness):
    surface = bed + water
    east_new = face_update(
        surface[:, :-1],
        surface[:, 1:],
        bed[:, :-1],
        bed[:, 1:],
        rough[:, :-1],
        rough[:, 1:],
        wetness[:, :-1],
        wetness[:, 1:],
        east[:, :-1],
    )
    south_new = face_update(
        surface[:-1],
        surface[1:],
        bed[:-1],
        bed[1:],
        rough[:-1],
        rough[1:],
        wetness[:-1],
        wetness[1:],
        south[:-1],
    )
    inner = water[1:-1, 1:-1] + TIME_STEP / SPACING * (
        east_new[1:-1, :-1] - east_new[1:-1, 1:] + south_new[:-1, 1:-1] - south_new[1:, 1:-1]
    )
    return jnp.stack([inner, east_new[1:-1, 1:], south_new[1:, 1:-1]])


def weir_flow(channel_level, plain_level, crest, factor, regime):
    upper = jnp.maximum(channel_level - crest, 0.0)
    lower = jnp.maximum(plain_level - crest, 0.0)
    free_flow = upper * jnp.sqrt(upper) - lower * jnp.sqrt(lower)
    drop = channel_level - plain_level
    drowned = drop * jnp.sqrt(jnp.abs(drop))
    return factor * jnp.where(regime == 1, free_flow, jnp.where(regime == 2, drowned, 0.0 * drop))


def compose(earlier, later):
    return (
        later[0] * earlier[0] + later[1] * earlier[2],
        later[0] * earlier[1] + later[1] * earlier[3],
        later[2] * earlier[0] + later[3] * earlier[2],
        later[2] * earlier[1] + later[3] * earlier[3],
        later[0] * earlier[4] + later[1] * earlier[5] + later[4],
        later[2] * earlier[4] + later[3] * earlier[5] + later[5],
    )


def on_device(
    water_depth,
    bed_level,
    roughness,
    wet_mask,
    flux_east,
    flux_south,
    bank_row,
    bank_column,
    link_section,
    link_reach,
    link_crest,
    link_factor,
    link_regime,
    channel_segment,
    old_discharge,
    courant,
    junction,
    pass_share,
    inflow,
):
    tile_rows, tile_cols = water_depth.shape
    reach_count = channel_segment.shape[1]
    devices = lax.axis_size(("gx", "gy"))
    capacity = bank_row.shape[0] // devices
    bank_cell = bank_row * tile_cols + bank_column
    plain_levels = (bed_level + water_depth).reshape(-1)[bank_cell].reshape(devices, capacity)
    arrived = lax.all_to_all(plain_levels, ("gx", "gy"), split_axis=0, concat_axis=0, tiled=True)
    section_index = (link_section * reach_count + link_reach).reshape(devices, capacity)
    channel_level = channel_segment.reshape(-1)[section_index]
    link_flow = weir_flow(
        channel_level,
        arrived,
        link_crest.reshape(devices, capacity),
        link_factor.reshape(devices, capacity),
        link_regime.reshape(devices, capacity),
    )
    lateral = (
        jnp.zeros((channel_segment.size,), jnp.float32)
        .at[section_index.reshape(-1)]
        .add(-link_flow.reshape(-1))
        .reshape(channel_segment.shape)
    )
    returned = lax.all_to_all(link_flow, ("gx", "gy"), split_axis=0, concat_axis=0, tiled=True)
    bank_gain = (
        jnp.zeros((tile_rows * tile_cols,), jnp.float32)
        .at[bank_cell]
        .add(returned.reshape(-1))
        .reshape(tile_rows, tile_cols)
    )
    scale = 0.5 + IMPLICIT_WEIGHT * courant
    passing = jnp.where(junction == 1, pass_share, 1.0 + 0.0 * pass_share)
    carry_weight = passing * (IMPLICIT_WEIGHT * courant - 0.5) / scale
    old_weight = passing * (0.5 + (1.0 - IMPLICIT_WEIGHT) * courant) / scale
    offset = (
        (0.5 - (1.0 - IMPLICIT_WEIGHT) * courant) * old_discharge
        + LATERAL_SCALE * courant * lateral
    ) / scale
    nothing = jnp.zeros_like(carry_weight)
    prefix = lax.associative_scan(
        compose, (carry_weight, old_weight, nothing, nothing, offset, old_discharge), axis=0
    )
    device_map = tuple((member[-1] for member in prefix))
    ones_lane = jnp.ones_like(inflow)
    zeros_lane = jnp.zeros_like(inflow)
    neutral = (ones_lane, zeros_lane, zeros_lane, ones_lane, zeros_lane, zeros_lane)
    static = jnp.stack([bed_level, roughness, wet_mask.astype(jnp.float32)])
    state = jnp.stack([water_depth, flux_east, flux_south])
    piece = with_halo(static, (("gx", 1), ("gy", 2)), 1)
    for index in range(SUBSTEPS):
        padded = with_halo(state, (("gx", 1), ("gy", 2)), 1)
        state = substep(padded[0], padded[1], padded[2], piece[0], piece[1], piece[2])
    before = entering(
        (device_map[0], device_map[1], device_map[2], device_map[3], device_map[4], device_map[5]),
        ("gx", "gy"),
        compose,
        neutral,
    )
    entering_new = before[0] * inflow + before[1] * inflow + before[4]
    entering_old = before[2] * inflow + before[3] * inflow + before[5]
    new_discharge = prefix[0] * entering_new + prefix[1] * entering_old + prefix[4]
    new_depth = state[0] + BANK_GAIN * bank_gain
    return (new_depth, state[1], state[2], new_discharge)


def solution(mesh):
    in_specs = (
        P("gx", "gy"),
        P("gx", "gy"),
        P("gx", "gy"),
        P("gx", "gy"),
        P("gx", "gy"),
        P("gx", "gy"),
        P(("gx", "gy")),
        P(("gx", "gy")),
        P(("gx", "gy")),
        P(("gx", "gy")),
        P(("gx", "gy")),
        P(("gx", "gy")),
        P(("gx", "gy")),
        P(("gx", "gy"), None),
        P(("gx", "gy"), None),
        P(("gx", "gy"), None),
        P(("gx", "gy"), None),
        P(("gx", "gy"), None),
        P(),
    )
    out_specs = (P("gx", "gy"), P("gx", "gy"), P("gx", "gy"), P(("gx", "gy"), None))
    return jax.shard_map(
        on_device, mesh=mesh, in_specs=in_specs, out_specs=out_specs, check_vma=False
    )
```

profile of v0, /device:TPU:1, one launch (start us, length us, event | category | flops | bytes accessed | tf_op | source)
XLA Modules:
  0.0 1319.4 jit_solution(8901056473199128799)
XLA Ops:
  0.6 0.8 pad_maximum_fusion.46
  1.5 3.3 collective-permute-start.1
  4.8 3.7 collective-permute-start
  8.6 2.1 collective-permute-start.5
  10.6 3.6 collective-permute-start.4
  14.5 1.3 collective-permute-start.3
  15.8 4.0 collective-permute-start.2
  19.9 1.3 collective-permute-start.7
  21.2 4.0 collective-permute-start.6
  25.2 0.2 pad_maximum_fusion
  25.5 1.0 collective-permute-done.7
  26.5 1.5 collective-permute-done.6
  28.0 0.2 pad_maximum_fusion.1
  28.3 0.2 fusion.12
  28.4 0.2 add_divide_fusion.3
  28.7 0.1 fusion.37
  28.8 2.5 collective-permute-start.9
  31.4 3.4 collective-permute-start.8
  34.9 0.6 collective-permute-done.8
  35.7 1.3 collective-permute-start.11
  37.0 4.7 collective-permute-start.10
  41.8 320.1 %gather_fusion.1 = f32[32768]{0:T(1024)} fusion(f32[16384]{0:T(1024)S(1)} %bitcast.174, s32[32768]{0:T(1024)S(1)} %get-tuple-element.132), kind=kCustom, calls=%fused_computation.1 | custom fusion | bytes 393216 | tf_op jit(solution)/shard_map/gather | solution.py:134
  361.9 16.8 %all-to-all-start = ((f32[128,1,256]{2,1,0:T(1,128)}), f32[128,1,256]{2,1,0:T(1,128)S(1)}, u32[]{:S(2)}, u32[]{:S(2)}) async-start(f32[128,1,256]{2,1,0:T(1,128)} %bitcast.39), calls=%async_computation | async-start | bytes 262144 | tf_op jit(solution)/shard_map/all_to_all | solution.py:135
  378.7 0.2 pad_maximum_fusion.2
  379.1 0.2 add_divide_fusion.2
  379.5 3.1 collective-permute-start.13
  382.6 2.6 collective-permute-start.12
  385.3 0.6 collective-permute-done.12
  386.1 1.3 collective-permute-start.15
  387.4 4.0 collective-permute-start.14
  391.5 1.3 collective-permute-done.15
  392.8 0.9 collective-permute-done.14
  393.6 0.2 pad_maximum_fusion.3
  394.0 0.2 add_divide_fusion.1
  394.4 2.9 collective-permute-start.17
  397.3 3.8 collective-permute-start.16
  401.1 0.8 copy-done.7
  402.0 0.9 copy-done.5
  402.9 0.8 copy-done.14
  403.7 180.5 %gather_fusion = f32[32768]{0:T(1024)S(1)} fusion(f32[16384]{0:T(1024)S(1)} %bitcast.175, s32[32768]{0:T(1024)S(1)} %broadcast_clamp_fusion.1), kind=kCustom, calls=%fused_computation | custom fusion | bytes 393216 | tf_op jit(solution)/shard_map/gather | solution.py:137
  584.5 1.3 collective-permute-start.19
  585.8 4.7 collective-permute-start.18
  590.5 0.2 collective-permute-done.19
  590.7 1.8 collective-permute-done.18
  592.4 0.2 pad_maximum_fusion.4
  592.8 0.2 add_divide_fusion
  593.0 0.7 copy-done.12
  593.7 0.2 fusion.6
  593.9 171.1 %scatter_custom_fusion.1 = f32[16384]{0:T(1024)S(1)} fusion(s32[32768]{0:T(1024)S(1)} %get-tuple-element.119, f32[32768]{0:T(1024)S(1)} %get-tuple-element.116, f32[]{:T(128)} %constant.90.clone.1), kind=kCustom, calls=%fused_computation.156 | custom fusion | flops 32768 | bytes 65540 | tf_op jit(solution)/shard_map/scatter-add | solution.py:148
  765.0 0.8 copy-done.15
  768.3 0.2 fusion.2
  768.5 0.8 copy.25
  769.3 14.9 %all-to-all-start.1 = ((f32[128,1,256]{2,1,0:T(1,128)}), f32[128,1,256]{2,1,0:T(1,128)S(1)}, u32[]{:S(2)}, u32[]{:S(2)}) async-start(f32[128,1,256]{2,1,0:T(1,128)} %copy.25), calls=%async_computation.1 | async-start | bytes 262144 | tf_op jit(solution)/shard_map/all_to_all | solution.py:151
  785.0 61.8 %all-gather = f32[128,1,512]{2,1,0:T(1,128)S(1)} all-gather(f32[1,1,512]{2,1,0:T(1,128)S(1)} %add_bitcast_fusion.3), channel_id=1, replica_groups=mesh['gx'=8,'gy'=16] {'gx','gy'}, dimensions={0}, use_global_device_ids=true | all-gather | bytes 264192 | tf_op jit(solution)/shard_map/all_gather | solution.py:33
  846.9 59.6 %all-gather.1 = f32[128,1,512]{2,1,0:T(1,128)S(1)} all-gather(f32[1,1,512]{2,1,0:T(1,128)S(1)} %add_bitcast_fusion.2), channel_id=1, replica_groups=mesh['gx'=8,'gy'=16] {'gx','gy'}, dimensions={0}, use_global_device_ids=true | all-gather | bytes 264192 | tf_op jit(solution)/shard_map/all_gather | solution.py:33
  906.6 59.4 %all-gather.2 = f32[128,1,512]{2,1,0:T(1,128)S(1)} all-gather(f32[1,1,512]{2,1,0:T(1,128)S(1)} %get-tuple-element.250), channel_id=1, replica_groups=mesh['gx'=8,'gy'=16] {'gx','gy'}, dimensions={0}, use_global_device_ids=true | all-gather | bytes 264192 | tf_op jit(solution)/shard_map/all_gather | solution.py:33
  966.0 59.4 %all-gather.3 = f32[128,1,512]{2,1,0:T(1,128)S(1)} all-gather(f32[1,1,512]{2,1,0:T(1,128)S(1)} %get-tuple-element.249), channel_id=1, replica_groups=mesh['gx'=8,'gy'=16] {'gx','gy'}, dimensions={0}, use_global_device_ids=true | all-gather | bytes 264192 | tf_op jit(solution)/shard_map/all_gather | solution.py:33
  1025.5 59.4 %all-gather.4 = f32[128,1,512]{2,1,0:T(1,128)S(1)} all-gather(f32[1,1,512]{2,1,0:T(1,128)S(1)} %add_bitcast_fusion.1), channel_id=1, replica_groups=mesh['gx'=8,'gy'=16] {'gx','gy'}, dimensions={0}, use_global_device_ids=true | all-gather | bytes 264192 | tf_op jit(solution)/shard_map/all_gather | solution.py:33
  1084.9 59.4 %all-gather.5 = f32[128,1,512]{2,1,0:T(1,128)S(1)} all-gather(f32[1,1,512]{2,1,0:T(1,128)S(1)} %get-tuple-element.248), channel_id=1, replica_groups=mesh['gx'=8,'gy'=16] {'gx','gy'}, dimensions={0}, use_global_device_ids=true | all-gather | bytes 264192 | tf_op jit(solution)/shard_map/all_gather | solution.py:33
  1144.4 1.7 while.20
  1146.2 0.7 copy-done.18
  1146.8 0.7 add_add_fusion.2
  1147.5 171.1 %scatter_custom_fusion = f32[16384]{0:T(1024)S(1)} fusion(s32[32768]{0:T(1024)S(1)} %get-tuple-element.133, f32[32768]{0:T(1024)S(1)} %bitcast.205, f32[]{:T(128)} %constant.90.clone.1), kind=kCustom, calls=%fused_computation.158 | custom fusion | flops 32768 | bytes 65540 | tf_op jit(solution)/shard_map/scatter-add | solution.py:155
  1318.6 0.8 fusion.25
  (354 shorter events, 5.8 us)
Async XLA Ops:
  0.6 7.8 copy-start.13
  1.5 12.8 collective-permute-start.1
  4.8 3.7 copy-start
  4.8 3.7 copy-start.4
  4.8 9.5 collective-permute-start
  8.5 5.8 copy-start.1
  8.5 5.8 copy-start.2
  8.5 5.8 copy-start.3
  8.6 11.2 collective-permute-start.5
  10.6 9.1 collective-permute-start.4
  14.5 10.8 collective-permute-start.3
  15.8 9.5 collective-permute-start.2
  19.9 6.6 collective-permute-start.7
  21.2 6.8 collective-permute-start.6
  28.7 6.2 copy-start.9
  28.8 6.0 copy-start.8
  28.8 6.1 collective-permute-start.9
  31.4 4.2 collective-permute-start.8
  35.7 343.0 %collective-permute-start.11 = (f32[3,66,1]{2,1,0:T(8,128)S(1)}, f32[3,66,1]{2,1,0:T(8,128)S(1)}, u32[]{:S(2)}, u32[]{:S(2)}) collective-permute-start(f32[3,66,1]{2,1,0:T(8,128)S(1)} %get-tuple-element.162), channel_id=1, source_target_pairs={{1,0},{2,1},{3,2},{4,3},{5,4},{6,5},{7,6},{8,7},{9,8},{10,9},{11,1... | collective-permute-start | bytes 2384 | tf_op jit(solution)/shard_map/ppermute | solution.py:26
  37.0 341.7 %collective-permute-start.10 = (f32[3,66,1]{2,1,0:T(8,128)S(1)}, f32[3,66,1]{2,1,0:T(8,128)S(1)}, u32[]{:S(2)}, u32[]{:S(2)}) collective-permute-start(f32[3,66,1]{2,1,0:T(8,128)S(1)} %get-tuple-element.161), channel_id=1, source_target_pairs={{0,1},{1,2},{2,3},{3,4},{4,5},{5,6},{6,7},{7,8},{8,9},{9,10},{10,1... | collective-permute-start | bytes 2384 | tf_op jit(solution)/shard_map/ppermute | solution.py:25
  361.9 231.2 %all-to-all-start = ((f32[128,1,256]{2,1,0:T(1,128)}), f32[128,1,256]{2,1,0:T(1,128)S(1)}, u32[]{:S(2)}, u32[]{:S(2)}) async-start(f32[128,1,256]{2,1,0:T(1,128)} %bitcast.39), calls=%async_computation | async-start | bytes 262144 | tf_op jit(solution)/shard_map/all_to_all | solution.py:135
  379.3 5.9 copy-start.11
  379.4 5.8 copy-start.10
  379.5 5.8 collective-permute-start.13
  382.6 3.3 collective-permute-start.12
  386.1 6.7 collective-permute-start.15
  387.4 6.3 collective-permute-start.14
  394.4 189.9 %collective-permute-start.17 = (f32[3,1,256]{2,1,0:T(1,128)S(1)}, f32[3,1,256]{2,1,0:T(1,128)S(1)}, u32[]{:S(2)}, u32[]{:S(2)}) collective-permute-start(f32[3,1,256]{2,1,0:T(1,128)S(1)} %get-tuple-element.170), channel_id=1, source_target_pairs={{16,0},{32,16},{48,32},{64,48},{80,64},{96,80},{112,96},{17,1},{33... | collective-permute-start | bytes 9224 | tf_op jit(solution)/shard_map/ppermute | solution.py:26
  397.3 187.0 %collective-permute-start.16 = (f32[3,1,256]{2,1,0:T(1,128)S(1)}, f32[3,1,256]{2,1,0:T(1,128)S(1)}, u32[]{:S(2)}, u32[]{:S(2)}) collective-permute-start(f32[3,1,256]{2,1,0:T(1,128)S(1)} %get-tuple-element.169), channel_id=1, source_target_pairs={{0,16},{16,32},{32,48},{48,64},{64,80},{80,96},{96,112},{1,17},{17... | collective-permute-start | bytes 9224 | tf_op jit(solution)/shard_map/ppermute | solution.py:25
  401.1 0.8 copy-start.7
  401.9 0.9 copy-start.5
  402.8 0.8 copy-start.14
  584.4 6.1 copy-start.6
  584.5 6.2 collective-permute-start.19
  585.8 6.7 collective-permute-start.18
  592.6 172.4 %copy-start.17 = (s32[32,512]{1,0:T(8,128)S(1)}, s32[32,512]{1,0:T(8,128)}, u32[]{:S(2)}) copy-start(s32[32,512]{1,0:T(8,128)} %param.37) | copy-start | bytes 196612
  592.8 0.9 copy-start.12
  765.0 0.8 copy-start.15
  765.0 0.9 copy-start.16
  769.3 378.2 %all-to-all-start.1 = ((f32[128,1,256]{2,1,0:T(1,128)}), f32[128,1,256]{2,1,0:T(1,128)S(1)}, u32[]{:S(2)}, u32[]{:S(2)}) async-start(f32[128,1,256]{2,1,0:T(1,128)} %copy.25), calls=%async_computation.1 | async-start | bytes 262144 | tf_op jit(solution)/shard_map/all_to_all | solution.py:151
  1146.1 0.7 copy-start.18
where the time goes:
time: 1330 us; the launch traced here: 1320 us
  local copies, waits for them, and re-layouts  510 us (38%)
  blocking collectives  359 us (27%)
  other arithmetic  349 us (26%)
  starting transfers between devices  90.6 us (7%)
    all_gather x6, blocking collectives, entering(): gathered = jax.tree.map(lambda a: lax.all_gather(a, axis), part)  359 us
    gather x1, local copies, waits for them, and re-layouts, on_device(): (bed_level + water_depth).reshape(-1)[bank_cell].reshape(devices, capacity)  320 us
    gather x2, local copies, waits for them, and re-layouts, on_device(): channel_level = channel_segment.reshape(-1)[section_index]  181 us
    scatter-add x1, other arithmetic, on_device(): lateral = jnp.zeros((channel_segment.size,), jnp.float32).at[section_inde...  171 us
    scatter-add x1, other arithmetic, on_device(): bank_gain = jnp.zeros((tile_rows * tile_cols,), jnp.float32).at[bank_cell...  171 us
    ppermute x10, starting transfers between devices, with_halo(): before = lax.ppermute(last, axis, up)  38.5 us
  transfers between devices with their start and end apart: 22, of which 8 were waited for; matrix products, arithmetic and copies ran while one was open for 38% of the time, Pallas kernels for 0%

commit v1 on v0

v1 whole, which is shorter than its diff:
```python
import functools

import jax
import jax.numpy as jnp
from jax import lax
from jax.experimental import pallas as pl
from jax.experimental.pallas import tpu as pltpu
from jax.sharding import PartitionSpec as P

GRAVITY = 9.81
SPACING = 20.0
TIME_STEP = 2.2
MIN_FLOW_DEPTH = 0.3
IMPLICIT_WEIGHT = 0.6
LATERAL_SCALE = 0.01
BANK_GAIN = 0.5
SUBSTEPS = 4

f32, bf16, i32, i16 = jnp.float32, jnp.bfloat16, jnp.int32, jnp.int16
MESH = pl.DeviceIdType.MESH

NGX, NGY = 8, 16
CX, CY = 64, 256
SEC, RIV = 32, 512
ROWS = 256
G = 64
PX, PY = CX + 8, CY + 128
STRIP = 8


def split2(x):
    hi = x.astype(bf16)
    return hi, (x - hi.astype(f32)).astype(bf16)


def one_hot(index_row, width):
    iota = lax.broadcasted_iota(i16, (width, 128), 0)
    index = jnp.broadcast_to(index_row.astype(i16), (width, 128))
    return jnp.where(iota == index, jnp.ones((), bf16), jnp.zeros((), bf16))


def gather_chunk(table, rows, cols):
    iota = lax.broadcasted_iota(i32, (64, 128), 0)
    picks = jnp.concatenate([one_hot(c, 256) for c in cols], 1)
    both = jnp.dot(table, picks, preferred_element_type=f32)
    both = both[:64] + both[64:]
    out = []
    for j, r in enumerate(rows):
        part = both[:, j * 128 : (j + 1) * 128]
        out.append(jnp.sum(jnp.where(iota == r, part, 0.0), 0, keepdims=True))
    return out


def scatter_chunk(flows, rows, cols):
    iota = lax.broadcasted_iota(i16, (64, 128), 0)
    zero = jnp.zeros((), bf16)
    picks = jnp.concatenate([one_hot(c, 256) for c in cols], 1)
    parts = []
    for flow, r in zip(flows, rows):
        hi, lo = split2(flow)
        mask = iota == jnp.broadcast_to(r.astype(i16), (64, 128))
        parts.append(
            jnp.concatenate(
                [
                    jnp.where(mask, jnp.broadcast_to(hi, (64, 128)), zero),
                    jnp.where(mask, jnp.broadcast_to(lo, (64, 128)), zero),
                ],
                0,
            )
        )
    parts = jnp.concatenate(parts, 1)
    return lax.dot_general(
        picks, parts, (((1,), (1,)), ((), ())), preferred_element_type=f32
    )


def kernel(*refs):
    hbm = refs[:19]
    depth_out, east_out, south_out, river_out = refs[19:23]
    vm = refs[23:42]
    (
        level_send,
        level_mid,
        level_turn,
        level_here,
        link_channel,
        flow_out,
        flow_mid,
        flow_turn,
        flow_here,
        halo_up,
        halo_down,
        from_north,
        from_south,
        strip_east,
        strip_west,
        from_west,
        from_east,
        old_send,
        old_before,
        map_row,
        map_col,
        fields,
        in_sem,
        gy_send,
        gy_recv,
        gx_send,
        gx_recv,
        back_gx_send,
        back_gx_recv,
        back_gy_send,
        back_gy_recv,
        halo_send,
        halo_recv,
        map_gy_send,
        map_gy_recv,
        map_gx_send,
        map_gx_recv,
    ) = refs[42:]
    (
        water, bed, rough, wet, east, south, bank_row, bank_col, link_sec, link_reach,
        crest, factor, regime, channel, old, courant, junction, share, inflow,
    ) = vm

    gx, gy = lax.axis_index("gx"), lax.axis_index("gy")

    order = [0, 1, 6, 7, 2, 3, 4, 5, 14, 13, 8, 9, 10, 11, 12, 15, 16, 17, 18]
    loads = {k: pltpu.make_async_copy(hbm[k], vm[k], in_sem.at[k]) for k in range(19)}
    for k in order:
        loads[k].start()

    chain = gx * NGY + gy
    after = lax.rem(chain + 1, NGX * NGY)
    before = lax.rem(chain + NGX * NGY - 1, NGX * NGY)
    barrier = pltpu.get_barrier_semaphore()

    def greet(where):
        pl.semaphore_signal(barrier, inc=1, device_id=where, device_id_type=MESH)

    def greet_gy(j, c):
        greet((gx, lax.rem(gy + j, NGY)))
        return c

    def greet_gx(j, c):
        greet((lax.rem(gx + j, NGX), gy))
        return c

    lax.fori_loop(1, NGY, greet_gy, 0)
    lax.fori_loop(1, NGX, greet_gx, 0)
    greet((after // NGY, lax.rem(after, NGY)))
    greet((before // NGY, lax.rem(before, NGY)))

    for k in (0, 1, 6, 7):
        loads[k].wait()
    level_table = jnp.concatenate(split2(bed[...] + water[...]), 0)

    def bank_rows(i):
        base = pl.multiple_of(i * 8, 8)
        found = []
        for j in range(G):
            there = (j & 7) * 32 + (j // 16) * 2 + ((j >> 3) & 1)
            found.append(pl.ds(base + there, 1))
        return found

    def gather_bank(i, c):
        at = bank_rows(i)
        got = gather_chunk(
            level_table, [bank_row[a, :] for a in at], [bank_col[a, :] for a in at]
        )
        level_send[pl.ds(pl.multiple_of(i * G, G), G), :] = jnp.concatenate(got, 0)
        return c

    lax.fori_loop(0, ROWS // G, gather_bank, 0)

    for k in (2, 3, 4, 5, 14):
        loads[k].wait()
    planes = (water, east, south, bed, rough, wet)
    for f, ref in enumerate(planes):
        halo_up[f] = ref[0:8, :].astype(f32)
        halo_down[f] = ref[CX - 8 : CX, :].astype(f32)
    old_send[...] = old[SEC - 1 : SEC, :]

    pl.semaphore_wait(barrier, NGX + NGY)

    def rows_of(p, n):
        return pl.ds(pl.multiple_of(p * n, n), n)

    def remote(src, dst, send, recv, where):
        return pltpu.make_async_remote_copy(
            src_ref=src, dst_ref=dst, send_sem=send, recv_sem=recv,
            device_id=where, device_id_type=MESH,
        )

    def gy_copy(src, dst, n, send, recv, p):
        return remote(
            src.at[rows_of(p, n)], dst.at[rows_of(gy, n)], send.at[p], recv.at[gy], (gx, p)
        )

    def gy_arrival(src, dst, n, send, recv, p):
        return remote(
            src.at[rows_of(p, n)], dst.at[rows_of(p, n)], send.at[p], recv.at[p], (gx, p)
        )

    def gx_copy(src, dst, n, send, recv, p):
        return remote(
            src.at[rows_of(p, n)], dst.at[rows_of(gx, n)], send.at[p], recv.at[gx], (p, gy)
        )

    def gx_arrival(src, dst, n, send, recv, p):
        return remote(
            src.at[rows_of(p, n)], dst.at[rows_of(p, n)], send.at[p], recv.at[p], (p, gy)
        )

    def gy_all(what):
        def one(j, c):
            what(lax.rem(gy + j, NGY))
            return c

        lax.fori_loop(1, NGY, one, 0)

    def gx_all(what):
        def one(j, c):
            what(lax.rem(gx + j, NGX))
            return c

        lax.fori_loop(1, NGX, one, 0)

    level_gy = (level_send, level_mid, 16, gy_send, gy_recv)
    level_gx = (level_turn, level_here, 32, gx_send, gx_recv)
    flow_gx = (flow_out, flow_mid, 32, back_gx_send, back_gx_recv)
    flow_gy = (flow_turn, flow_here, 16, back_gy_send, back_gy_recv)

    gy_all(lambda p: gy_copy(*level_gy, p).start())
    level_mid[rows_of(gy, 16), :] = level_send[rows_of(gy, 16), :]

    north, south_to = lax.rem(gx + NGX - 1, NGX), lax.rem(gx + 1, NGX)
    west, east_to = lax.rem(gy + NGY - 1, NGY), lax.rem(gy + 1, NGY)
    up_copy = remote(halo_up, from_south, halo_send.at[0], halo_recv.at[0], (north, gy))
    down_copy = remote(halo_down, from_north, halo_send.at[1], halo_recv.at[1], (south_to, gy))
    old_copy = remote(
        old_send, old_before, halo_send.at[4], halo_recv.at[4],
        (after // NGY, lax.rem(after, NGY)),
    )
    up_copy.start()
    down_copy.start()
    old_copy.start()

    for k in (13, 8, 9):
        loads[k].wait()
    channel_table = jnp.concatenate(
        split2(jnp.concatenate([channel[:, :CY], channel[:, CY:]], 0)), 0
    )

    def link_cells(i):
        base = pl.multiple_of(i * G, G)
        reach = [link_reach[pl.ds(base + j, 1), :] for j in range(G)]
        rows = [link_sec[pl.ds(base + j, 1), :] + ((q >> 8) << 5) for j, q in enumerate(reach)]
        return base, rows, [q & 255 for q in reach]

    def gather_channel(i, c):
        base, rows, cols = link_cells(i)
        link_channel[pl.ds(base, G), :] = jnp.concatenate(
            gather_chunk(channel_table, rows, cols), 0
        )
        return c

    lax.fori_loop(0, 2, gather_channel, 0)

    gy_all(lambda p: gy_arrival(*level_gy, p).wait_recv())
    for g in range(NGX):
        for k in range(4):
            level_turn[g * 32 + k * 8 : g * 32 + k * 8 + 8, :] = level_mid[
                pl.ds(g + 64 * k, 8, stride=8), :
            ]
    gx_all(lambda p: gx_copy(*level_gx, p).start())
    level_here[rows_of(gx, 32), :] = level_turn[rows_of(gx, 32), :]

    up_copy.wait_recv()
    down_copy.wait_recv()
    sub8 = lax.broadcasted_iota(i32, (8, CY), 0)
    lane = lax.broadcasted_iota(i32, (PX, 128), 1)
    pack_east = jnp.zeros((PX, 128), f32)
    pack_west = jnp.zeros((PX, 128), f32)
    for f, ref in enumerate(planes):
        beyond = jnp.where(
            sub8 < 4,
            jnp.where(gx < NGX - 1, from_south[f], 0.0),
            jnp.where(gx > 0, from_north[f], 0.0),
        )
        fields[f, 0:CX, 0:CY] = ref[...].astype(f32)
        fields[f, CX:PX, 0:CY] = beyond
        right = jnp.concatenate([ref[:, CY - 128 :].astype(f32), beyond[:, CY - 128 :]], 0)
        left = jnp.concatenate([ref[:, :128].astype(f32), beyond[:, :128]], 0)
        mine = (lane >= STRIP * f) & (lane < STRIP * f + 4)
        right = pltpu.roll(right, (STRIP * f + 4) % 128, 1)
        left = pltpu.roll(left, STRIP * f, 1) if f else left
        pack_east = jnp.where(mine, right, pack_east)
        pack_west = jnp.where(mine, left, pack_west)
    strip_east[...] = pack_east
    strip_west[...] = pack_west
    east_copy = remote(strip_east, from_west, halo_send.at[2], halo_recv.at[2], (gx, east_to))
    west_copy = remote(strip_west, from_east, halo_send.at[3], halo_recv.at[3], (gx, west))
    east_copy.start()
    west_copy.start()

    lax.fori_loop(2, 4, gather_channel, 0)

    for k in (10, 11, 12):
        loads[k].wait()
    gx_all(lambda p: gx_arrival(*level_gx, p).wait_recv())

    def flow_part(i, c):
        at = pl.ds(pl.multiple_of(i * 32, 32), 32)
        plain, chan, top, rule = level_here[at, :], link_channel[at, :], crest[at, :], regime[at, :]
        upper = jnp.maximum(chan - top, 0.0)
        lower = jnp.maximum(plain - top, 0.0)
        free = upper * jnp.sqrt(upper) - lower * jnp.sqrt(lower)
        drop = chan - plain
        drowned = drop * jnp.sqrt(jnp.abs(drop))
        flow_out[at, :] = factor[at, :] * jnp.where(
            rule == 1, free, jnp.where(rule == 2, drowned, 0.0)
        )
        return c

    lax.fori_loop(0, 8, flow_part, 0)
    gx_all(lambda p: gx_copy(*flow_gx, p).start())
    flow_mid[rows_of(gx, 32), :] = flow_out[rows_of(gx, 32), :]

    def scatter_lateral(i, acc):
        base, rows, cols = link_cells(i)
        return acc + scatter_chunk(
            [flow_out[pl.ds(base + j, 1), :] for j in range(G)], rows, cols
        )

    acc = lax.fori_loop(0, 2, scatter_lateral, jnp.zeros((CY, 128), f32))

    gx_all(lambda p: gx_arrival(*flow_gx, p).wait_recv())
    for g in range(NGY):
        for h in range(2):
            flow_turn[g * 16 + h * 8 : g * 16 + h * 8 + 8, :] = flow_mid[
                pl.ds(g * 2 + h, 8, stride=32), :
            ]
    gy_all(lambda p: gy_copy(*flow_gy, p).start())
    flow_here[rows_of(gy, 16), :] = flow_turn[rows_of(gy, 16), :]

    acc = lax.fori_loop(2, 4, scatter_lateral, acc).T
    acc = acc[:64] + acc[64:]
    lateral = -jnp.concatenate([acc[:SEC], acc[SEC:]], 1)

    for k in (15, 16, 17, 18):
        loads[k].wait()
    old_copy.wait_recv()
    cour = courant[...]
    inverse = 1.0 / (0.5 + IMPLICIT_WEIGHT * cour)
    passing = jnp.where(junction[...] == 1, share[...], 1.0)
    carry = passing * (IMPLICIT_WEIGHT * cour - 0.5) * inverse
    old_weight = passing * (0.5 + (1.0 - IMPLICIT_WEIGHT) * cour) * inverse
    here = old[...]
    sub = lax.broadcasted_iota(i32, (SEC, RIV), 0)
    previous = jnp.where(
        sub == 0,
        jnp.where(chain == 0, inflow[...], old_before[...]),
        pltpu.roll(here, 1, 0),
    )
    shift = old_weight * previous + (
        (0.5 - (1.0 - IMPLICIT_WEIGHT) * cour) * here + LATERAL_SCALE * cour * lateral
    ) * inverse
    step = 1
    while step < SEC:
        keep = sub >= step
        shift = jnp.where(keep, carry * pltpu.roll(shift, step, 0) + shift, shift)
        carry = jnp.where(keep, carry * pltpu.roll(carry, step, 0), carry)
        step *= 2
    total = jnp.concatenate([carry[SEC - 1 :], shift[SEC - 1 :]], 0)
    map_row[pl.ds(gy, 1)] = total[None]

    def map_gy(p, slot):
        return remote(
            map_row.at[gy], map_row.at[slot], map_gy_send.at[p], map_gy_recv.at[slot], (gx, p)
        )

    def map_gx(p, slot):
        return remote(
            map_col.at[gx], map_col.at[slot], map_gx_send.at[p], map_gx_recv.at[slot], (p, gy)
        )

    gy_all(lambda p: map_gy(p, gy).start())

    east_copy.wait_recv()
    west_copy.wait_recv()
    held = []
    for f in range(6):
        right = pltpu.roll(from_east[...], (128 - STRIP * f) % 128, 1) if f else from_east[...]
        left = pltpu.roll(from_west[...], (128 - STRIP * f - 4) % 128, 1)
        side = jnp.where(
            lane < 4,
            jnp.where(gy < NGY - 1, right, 0.0),
            jnp.where((lane >= 124) & (gy > 0), left, 0.0),
        )
        fields[f, :, CY:PY] = side
        held.append(fields[f])
    depth, q_east, q_south, ground, manning, wetness = held

    def of_east(a):
        return pltpu.roll(a, PY - 1, 1)

    def of_south(a):
        return pltpu.roll(a, PX - 1, 0)

    faces = []
    for move in (of_east, of_south):
        mean = 0.5 * (manning + move(manning))
        faces.append(
            (
                move,
                jnp.maximum(ground, move(ground)),
                GRAVITY * TIME_STEP * mean * mean,
                wetness * move(wetness),
            )
        )
    flux = [q_east, q_south]
    for _ in range(SUBSTEPS):
        surface = ground + depth
        for n, (move, top, rub, open_) in enumerate(faces):
            beside = move(surface)
            flow_depth = jnp.maximum(jnp.maximum(surface, beside) - top, MIN_FLOW_DEPTH)
            drive = flux[n] - (GRAVITY * TIME_STEP / SPACING) * flow_depth * (beside - surface)
            friction = 1.0 + rub * jnp.abs(flux[n]) * jnp.exp((-7.0 / 3.0) * jnp.log(flow_depth))
            flux[n] = open_ * drive / friction
        depth = depth + (TIME_STEP / SPACING) * (
            pltpu.roll(flux[0], 1, 1) - flux[0] + pltpu.roll(flux[1], 1, 0) - flux[1]
        )
    east_out[...] = flux[0][:CX, :CY]
    south_out[...] = flux[1][:CX, :CY]
    fields[0] = depth

    gy_all(lambda p: gy_arrival(*flow_gy, p).wait_recv())

    def scatter_bank(i, acc):
        at = bank_rows(i)
        base = pl.multiple_of(i * G, G)
        return acc + scatter_chunk(
            [flow_here[pl.ds(base + j, 1), :] for j in range(G)],
            [bank_row[a, :] for a in at],
            [bank_col[a, :] for a in at],
        )

    acc = lax.fori_loop(0, 1, scatter_bank, jnp.zeros((CY, 128), f32))

    gy_all(lambda p: map_gy(p, p).wait_recv())
    a_run, s_run = jnp.ones((1, RIV), f32), jnp.zeros((1, RIV), f32)
    a_in, s_in = a_run, s_run
    for j in range(NGY):
        a_in = jnp.where(j < gy + 1, a_run, a_in)
        s_in = jnp.where(j < gy + 1, s_run, s_in)
        a_j, s_j = map_row[j, 0:1, :], map_row[j, 1:2, :]
        s_run = a_j * s_run + s_j
        a_run = a_j * a_run
    map_col[pl.ds(gx, 1)] = jnp.concatenate([a_run, s_run], 0)[None]
    gx_all(lambda p: map_gx(p, gx).start())

    acc = lax.fori_loop(1, 4, scatter_bank, acc).T
    depth_out[...] = fields[0, 0:CX, 0:CY] + BANK_GAIN * (acc[:64] + acc[64:])

    gx_all(lambda p: map_gx(p, p).wait_recv())
    x = inflow[...]
    for j in range(NGX - 1):
        x = jnp.where(j < gx, map_col[j, 0:1, :] * x + map_col[j, 1:2, :], x)
    x = a_in * x + s_in
    river_out[...] = carry * x + shift

    gy_all(lambda p: gy_copy(*level_gy, p).wait_send())
    gx_all(lambda p: gx_copy(*level_gx, p).wait_send())
    gx_all(lambda p: gx_copy(*flow_gx, p).wait_send())
    gy_all(lambda p: gy_copy(*flow_gy, p).wait_send())
    gy_all(lambda p: map_gy(p, gy).wait_send())
    gx_all(lambda p: map_gx(p, gx).wait_send())
    for copy in (up_copy, down_copy, old_copy, east_copy, west_copy):
        copy.wait_send()


def on_device(*args):
    args = list(args)
    for k in range(6, 13):
        args[k] = args[k].reshape(ROWS, 128)
    args[18] = args[18].reshape(1, RIV)
    link = pltpu.VMEM((ROWS, 128), f32)
    halo_rows = pltpu.VMEM((6, 8, CY), f32)
    strip = pltpu.VMEM((PX, 128), f32)
    dma = pltpu.SemaphoreType.DMA
    scratch = [pltpu.VMEM(a.shape, a.dtype) for a in args]
    scratch += [link] * 9
    scratch += [halo_rows] * 4
    scratch += [strip] * 4
    scratch += [pltpu.VMEM((1, RIV), f32)] * 2
    scratch += [pltpu.VMEM((NGY, 2, RIV), f32), pltpu.VMEM((NGX, 2, RIV), f32)]
    scratch += [pltpu.VMEM((6, PX, PY), f32)]
    scratch += [dma((19,))]
    scratch += [dma((NGY,)), dma((NGY,)), dma((NGX,)), dma((NGX,))]
    scratch += [dma((NGX,)), dma((NGX,)), dma((NGY,)), dma((NGY,))]
    scratch += [dma((5,)), dma((5,))]
    scratch += [dma((NGY,)), dma((NGY,)), dma((NGX,)), dma((NGX,))]
    return pl.pallas_call(
        kernel,
        out_shape=(
            jax.ShapeDtypeStruct((CX, CY), f32),
            jax.ShapeDtypeStruct((CX, CY), f32),
            jax.ShapeDtypeStruct((CX, CY), f32),
            jax.ShapeDtypeStruct((SEC, RIV), f32),
        ),
        in_specs=[pl.BlockSpec(memory_space=pl.ANY)] * 19,
        out_specs=[pl.BlockSpec(memory_space=pltpu.VMEM)] * 4,
        scratch_shapes=scratch,
        compiler_params=pltpu.CompilerParams(
            collective_id=0, has_side_effects=True, vmem_limit_bytes=48 << 20
        ),
        cost_estimate=pl.CostEstimate(
            flops=8 * 10**9, bytes_accessed=2 * 10**6, transcendentals=10**6
        ),
        name="coupled_step",
    )(*args)


def solution(mesh):
    tile, flat, chain = P("gx", "gy"), P(("gx", "gy")), P(("gx", "gy"), None)
    in_specs = (tile,) * 6 + (flat,) * 7 + (chain,) * 5 + (P(),)
    out_specs = (tile, tile, tile, chain)
    return jax.shard_map(
        on_device, mesh=mesh, in_specs=in_specs, out_specs=out_specs, check_vma=False
    )
```

time: 1330 us -> 58.3 us (0.04)
  local copies, waits for them, and re-layouts: 510 us -> 18.7 us
  blocking collectives: 359 us -> 0 us
  other arithmetic: 349 us -> 0 us
  starting transfers between devices: 90.6 us -> 0 us
  Pallas kernels: 0 us -> 38.1 us
    gather x3 -> x0, local copies, waits for them, and re-layouts: 501 us -> none  [the longest x1 320 us: on_device(): (bed_level + water_depth).reshape(-1)[bank_cell].reshape(devices, capacity)]
    all_gather x6 -> x0, blocking collectives: 359 us -> none  [entering(): gathered = jax.tree.map(lambda a: lax.all_gather(a, axis), part)]
    scatter-add x2 -> x0, other arithmetic: 342 us -> none  [the longest x1 171 us: on_device(): lateral = jnp.zeros((channel_segment.size,), jnp.float32).at[section_inde...]
    ppermute x20 -> x0, starting transfers between devices: 58.9 us -> none  [the longest x10 38.5 us: with_halo(): before = lax.ppermute(last, axis, up)]
    pallas_call x0 -> x1, Pallas kernels: none -> 38.1 us  [on_device(): pl.pallas_call(kernel, out_shape=(jax.ShapeDtypeStruct((CX, CY), f32), ja...]
    all_to_all x2 -> x0, starting transfers between devices: 31.8 us -> none  [the longest x1 16.8 us: on_device(): lax.all_to_all(plain_levels, ('gx', 'gy'), split_axis=0, concat_axis=0, t...]
    unnamed x50 -> x42, local copies, waits for them, and re-layouts: 5 us -> 18.7 us
  transfers between devices with their start and end apart: 22 -> 0, of which waited for: 8 -> 0; matrix products, arithmetic and copies ran while one was open for 38% -> 0% of each run, Pallas kernels for 0% -> 0%
where the time goes in v1:
time: 58.3 us; the launch traced here: 57.5 us
  Pallas kernels  38.1 us (65%)
  local copies, waits for them, and re-layouts  18.7 us (32%)
  between operations  0.68 us (1%)
    pallas_call x1, Pallas kernels, on_device(): pl.pallas_call(kernel, out_shape=(jax.ShapeDtypeStruct((CX, CY), f32), ja...  38.1 us
    unnamed x42, local copies, waits for them, and re-layouts  18.7 us

profile of v1, /device:TPU:1, one launch (start us, length us, event | category | flops | bytes accessed | tf_op | source)
XLA Modules:
  0.0 57.5 jit_solution(2587845689642569646)
XLA Ops:
  0.6 0.0 copy-start.18
  0.6 0.7 %copy-done.18 = f32[512]{0:T(512)S(1)} copy-done((f32[512]{0:T(512)S(1)}, f32[512]{0:T(512)}, u32[]{:S(2)}) %copy-start.18) | copy-done | bytes 2072
  1.3 0.0 copy-start
  1.3 0.9 %copy-done = s32[32768]{0:T(1024)S(1)} copy-done((s32[32768]{0:T(1024)S(1)}, s32[32768]{0:T(1024)}, u32[]{:S(2)}) %copy-start) | copy-done | bytes 131096
  2.2 0.0 copy-start.1
  2.2 0.9 %copy-done.1 = s32[32768]{0:T(1024)S(1)} copy-done((s32[32768]{0:T(1024)S(1)}, s32[32768]{0:T(1024)}, u32[]{:S(2)}) %copy-start.1) | copy-done | bytes 131096
  3.1 0.0 copy-start.2
  3.1 0.9 %copy-done.2 = s32[32768]{0:T(1024)S(1)} copy-done((s32[32768]{0:T(1024)S(1)}, s32[32768]{0:T(1024)}, u32[]{:S(2)}) %copy-start.2) | copy-done | bytes 131096
  4.0 0.0 copy-start.3
  4.0 0.9 %copy-done.3 = s32[32768]{0:T(1024)S(1)} copy-done((s32[32768]{0:T(1024)S(1)}, s32[32768]{0:T(1024)}, u32[]{:S(2)}) %copy-start.3) | copy-done | bytes 131096
  4.9 0.0 copy-start.4
  4.9 0.9 %copy-done.4 = f32[32768]{0:T(1024)S(1)} copy-done((f32[32768]{0:T(1024)S(1)}, f32[32768]{0:T(1024)}, u32[]{:S(2)}) %copy-start.4) | copy-done | bytes 131096
  5.8 0.0 copy-start.5
  5.8 0.9 %copy-done.5 = f32[32768]{0:T(1024)S(1)} copy-done((f32[32768]{0:T(1024)S(1)}, f32[32768]{0:T(1024)}, u32[]{:S(2)}) %copy-start.5) | copy-done | bytes 131096
  6.8 0.0 copy-start.6
  6.8 0.9 %copy-done.6 = s32[32768]{0:T(1024)S(1)} copy-done((s32[32768]{0:T(1024)S(1)}, s32[32768]{0:T(1024)}, u32[]{:S(2)}) %copy-start.6) | copy-done | bytes 131096
  7.7 0.0 copy-start.7
  7.7 0.8 %copy-done.7 = f32[64,256]{1,0:T(8,128)S(1)} copy-done((f32[64,256]{1,0:T(8,128)S(1)}, f32[64,256]{1,0:T(8,128)}, u32[]{:S(2)}) %copy-start.7) | copy-done | bytes 65560
  8.5 0.0 copy-start.8
  8.5 0.8 %copy-done.8 = f32[64,256]{1,0:T(8,128)S(1)} copy-done((f32[64,256]{1,0:T(8,128)S(1)}, f32[64,256]{1,0:T(8,128)}, u32[]{:S(2)}) %copy-start.8) | copy-done | bytes 65560
  9.3 0.0 copy-start.9
  9.3 0.8 %copy-done.9 = f32[64,256]{1,0:T(8,128)S(1)} copy-done((f32[64,256]{1,0:T(8,128)S(1)}, f32[64,256]{1,0:T(8,128)}, u32[]{:S(2)}) %copy-start.9) | copy-done | bytes 65560
  10.2 0.0 copy-start.10
  10.2 0.8 %copy-done.10 = s32[64,256]{1,0:T(8,128)S(1)} copy-done((s32[64,256]{1,0:T(8,128)S(1)}, s32[64,256]{1,0:T(8,128)}, u32[]{:S(2)}) %copy-start.10) | copy-done | bytes 65560
  11.0 0.0 copy-start.11
  11.0 0.8 %copy-done.11 = f32[64,256]{1,0:T(8,128)S(1)} copy-done((f32[64,256]{1,0:T(8,128)S(1)}, f32[64,256]{1,0:T(8,128)}, u32[]{:S(2)}) %copy-start.11) | copy-done | bytes 65560
  11.9 0.0 copy-start.12
  11.9 0.8 %copy-done.12 = f32[64,256]{1,0:T(8,128)S(1)} copy-done((f32[64,256]{1,0:T(8,128)S(1)}, f32[64,256]{1,0:T(8,128)}, u32[]{:S(2)}) %copy-start.12) | copy-done | bytes 65560
  12.7 0.0 copy-start.13
  12.7 0.8 %copy-done.13 = f32[32,512]{1,0:T(8,128)S(1)} copy-done((f32[32,512]{1,0:T(8,128)S(1)}, f32[32,512]{1,0:T(8,128)}, u32[]{:S(2)}) %copy-start.13) | copy-done | bytes 65560
  13.5 0.0 copy-start.14
  13.5 0.8 %copy-done.14 = f32[32,512]{1,0:T(8,128)S(1)} copy-done((f32[32,512]{1,0:T(8,128)S(1)}, f32[32,512]{1,0:T(8,128)}, u32[]{:S(2)}) %copy-start.14) | copy-done | bytes 65560
  14.4 0.0 copy-start.15
  14.4 0.8 %copy-done.15 = f32[32,512]{1,0:T(8,128)S(1)} copy-done((f32[32,512]{1,0:T(8,128)S(1)}, f32[32,512]{1,0:T(8,128)}, u32[]{:S(2)}) %copy-start.15) | copy-done | bytes 65560
  15.2 0.0 copy-start.16
  15.2 0.8 %copy-done.16 = s32[32,512]{1,0:T(8,128)S(1)} copy-done((s32[32,512]{1,0:T(8,128)S(1)}, s32[32,512]{1,0:T(8,128)}, u32[]{:S(2)}) %copy-start.16) | copy-done | bytes 65560
  16.1 0.0 copy-start.17
  16.1 0.8 %copy-done.17 = f32[32,512]{1,0:T(8,128)S(1)} copy-done((f32[32,512]{1,0:T(8,128)S(1)}, f32[32,512]{1,0:T(8,128)}, u32[]{:S(2)}) %copy-start.17) | copy-done | bytes 65560
  16.9 38.1 %coupled_step.1 = (f32[64,256]{1,0:T(8,128)S(1)}, f32[64,256]{1,0:T(8,128)S(1)}, f32[64,256]{1,0:T(8,128)S(1)}, f32[32,512]{1,0:T(8,128)S(1)}) custom-call(f32[64,256]{1,0:T(8,128)S(1)} %copy-done.7, f32[64,256]{1,0:T(8,128)S(1)} %copy-done.8, f32[64,256]{1,0:T(8,128)S(1)} %copy-done.9, s32[64,256]{1,0:T(8,128)S(1)} %copy-done.10, f32[64,256]{1,0:T(8,128)S(1)} %copy-done.11, ...), custom_call_target="tpu_custom_call" | custom-call | flops 8000000000 | bytes 2000000 | tf_op jit(solution)/shard_map/coupled_step/pallas_call | solution.py:503
  55.0 0.6 %copy.27 = f32[64,256]{1,0:T(8,128)} copy(f32[64,256]{1,0:T(8,128)S(1)} %get-tuple-element.8) | data formatting | bytes 131072
  55.6 0.6 %copy.28 = f32[64,256]{1,0:T(8,128)} copy(f32[64,256]{1,0:T(8,128)S(1)} %get-tuple-element.9) | data formatting | bytes 131072
  56.2 0.6 %copy.29 = f32[64,256]{1,0:T(8,128)} copy(f32[64,256]{1,0:T(8,128)S(1)} %get-tuple-element.10) | data formatting | bytes 131072
  56.9 0.6 %copy.30 = f32[32,512]{1,0:T(8,128)} copy(f32[32,512]{1,0:T(8,128)S(1)} %get-tuple-element.11) | data formatting | bytes 131072
Async XLA Ops:
  0.6 0.7 %copy-start.18 = (f32[512]{0:T(512)S(1)}, f32[512]{0:T(512)}, u32[]{:S(2)}) copy-start(f32[512]{0:T(512)} %param.37) | copy-start | bytes 6148
  1.3 0.9 %copy-start = (s32[32768]{0:T(1024)S(1)}, s32[32768]{0:T(1024)}, u32[]{:S(2)}) copy-start(s32[32768]{0:T(1024)} %param.25) | copy-start | bytes 393220
  2.2 0.9 %copy-start.1 = (s32[32768]{0:T(1024)S(1)}, s32[32768]{0:T(1024)}, u32[]{:S(2)}) copy-start(s32[32768]{0:T(1024)} %param.26) | copy-start | bytes 393220
  3.1 0.9 %copy-start.2 = (s32[32768]{0:T(1024)S(1)}, s32[32768]{0:T(1024)}, u32[]{:S(2)}) copy-start(s32[32768]{0:T(1024)} %param.27) | copy-start | bytes 393220
  4.0 0.9 %copy-start.3 = (s32[32768]{0:T(1024)S(1)}, s32[32768]{0:T(1024)}, u32[]{:S(2)}) copy-start(s32[32768]{0:T(1024)} %param.28) | copy-start | bytes 393220
  4.9 0.9 %copy-start.4 = (f32[32768]{0:T(1024)S(1)}, f32[32768]{0:T(1024)}, u32[]{:S(2)}) copy-start(f32[32768]{0:T(1024)} %param.29) | copy-start | bytes 393220
  5.8 0.9 %copy-start.5 = (f32[32768]{0:T(1024)S(1)}, f32[32768]{0:T(1024)}, u32[]{:S(2)}) copy-start(f32[32768]{0:T(1024)} %param.30) | copy-start | bytes 393220
  6.8 0.9 %copy-start.6 = (s32[32768]{0:T(1024)S(1)}, s32[32768]{0:T(1024)}, u32[]{:S(2)}) copy-start(s32[32768]{0:T(1024)} %param.31) | copy-start | bytes 393220
  7.7 0.8 %copy-start.7 = (f32[64,256]{1,0:T(8,128)S(1)}, f32[64,256]{1,0:T(8,128)}, u32[]{:S(2)}) copy-start(f32[64,256]{1,0:T(8,128)} %refs_0_.1) | copy-start | bytes 196612
  8.5 0.8 %copy-start.8 = (f32[64,256]{1,0:T(8,128)S(1)}, f32[64,256]{1,0:T(8,128)}, u32[]{:S(2)}) copy-start(f32[64,256]{1,0:T(8,128)} %refs_1_.1) | copy-start | bytes 196612
  9.3 0.8 %copy-start.9 = (f32[64,256]{1,0:T(8,128)S(1)}, f32[64,256]{1,0:T(8,128)}, u32[]{:S(2)}) copy-start(f32[64,256]{1,0:T(8,128)} %refs_2_.1) | copy-start | bytes 196612
  10.2 0.8 %copy-start.10 = (s32[64,256]{1,0:T(8,128)S(1)}, s32[64,256]{1,0:T(8,128)}, u32[]{:S(2)}) copy-start(s32[64,256]{1,0:T(8,128)} %refs_3_.1) | copy-start | bytes 196612
  11.0 0.8 %copy-start.11 = (f32[64,256]{1,0:T(8,128)S(1)}, f32[64,256]{1,0:T(8,128)}, u32[]{:S(2)}) copy-start(f32[64,256]{1,0:T(8,128)} %refs_4_.1) | copy-start | bytes 196612
  11.9 0.8 %copy-start.12 = (f32[64,256]{1,0:T(8,128)S(1)}, f32[64,256]{1,0:T(8,128)}, u32[]{:S(2)}) copy-start(f32[64,256]{1,0:T(8,128)} %refs_5_.1) | copy-start | bytes 196612
  12.7 0.8 %copy-start.13 = (f32[32,512]{1,0:T(8,128)S(1)}, f32[32,512]{1,0:T(8,128)}, u32[]{:S(2)}) copy-start(f32[32,512]{1,0:T(8,128)} %refs_13_.1) | copy-start | bytes 196612
  13.5 0.8 %copy-start.14 = (f32[32,512]{1,0:T(8,128)S(1)}, f32[32,512]{1,0:T(8,128)}, u32[]{:S(2)}) copy-start(f32[32,512]{1,0:T(8,128)} %refs_14_.1) | copy-start | bytes 196612
  14.4 0.8 %copy-start.15 = (f32[32,512]{1,0:T(8,128)S(1)}, f32[32,512]{1,0:T(8,128)}, u32[]{:S(2)}) copy-start(f32[32,512]{1,0:T(8,128)} %refs_15_.1) | copy-start | bytes 196612
  15.2 0.8 %copy-start.16 = (s32[32,512]{1,0:T(8,128)S(1)}, s32[32,512]{1,0:T(8,128)}, u32[]{:S(2)}) copy-start(s32[32,512]{1,0:T(8,128)} %refs_16_.1) | copy-start | bytes 196612
  16.1 0.8 %copy-start.17 = (f32[32,512]{1,0:T(8,128)S(1)}, f32[32,512]{1,0:T(8,128)}, u32[]{:S(2)}) copy-start(f32[32,512]{1,0:T(8,128)} %refs_17_.1) | copy-start | bytes 196612

commit v2 on v1

v2 whole, which is shorter than its diff:
```python
import functools

import jax
import jax.numpy as jnp
from jax import lax
from jax.experimental import pallas as pl
from jax.experimental.pallas import tpu as pltpu
from jax.sharding import PartitionSpec as P

GRAVITY = 9.81
SPACING = 20.0
TIME_STEP = 2.2
MIN_FLOW_DEPTH = 0.3
IMPLICIT_WEIGHT = 0.6
LATERAL_SCALE = 0.01
BANK_GAIN = 0.5
SUBSTEPS = 4

f32, bf16, i32, i16 = jnp.float32, jnp.bfloat16, jnp.int32, jnp.int16
MESH = pl.DeviceIdType.MESH

NGX, NGY = 8, 16
CX, CY = 64, 256
SEC, RIV = 32, 512
ROWS = 256
G = 128
DEV = NGX * NGY
PX, PY = CX + 8, CY + 128
STRIP = 8
LANES = 128
PER = RIV // LANES


def far_first():
    steps = [
        (z, c, y, x) for z in range(4) for c in range(2) for y in range(4) for x in range(4)
    ][1:]
    far = lambda s: min(s[0], 4 - s[0]) + min(s[2], 4 - s[2]) + min(s[3], 4 - s[3]) + 0.3 * s[1]
    return sorted(steps, key=far, reverse=True)


STEPS = far_first()


def split2(x):
    hi = x.astype(bf16)
    return hi, (x - hi.astype(f32)).astype(bf16)


def one_hot(index_row, width):
    iota = lax.broadcasted_iota(i16, (width, 128), 0)
    index = jnp.broadcast_to(index_row.astype(i16), (width, 128))
    return jnp.where(iota == index, jnp.ones((), bf16), jnp.zeros((), bf16))


def gather_chunk(table, rows, cols):
    iota = lax.broadcasted_iota(i32, (64, 128), 0)
    picks = jnp.concatenate([one_hot(c, 256) for c in cols], 1)
    both = jnp.dot(table, picks, preferred_element_type=f32)
    both = both[:64] + both[64:]
    out = []
    for j, r in enumerate(rows):
        part = both[:, j * 128 : (j + 1) * 128]
        out.append(jnp.sum(jnp.where(iota == r, part, 0.0), 0, keepdims=True))
    return out


def scatter_chunk(flows, rows, cols):
    iota = lax.broadcasted_iota(i16, (64, 128), 0)
    zero = jnp.zeros((), bf16)
    picks = jnp.concatenate([one_hot(c, 256) for c in cols], 1)
    parts = []
    for flow, r in zip(flows, rows):
        hi, lo = split2(flow)
        mask = iota == jnp.broadcast_to(r.astype(i16), (64, 128))
        parts.append(
            jnp.concatenate(
                [
                    jnp.where(mask, jnp.broadcast_to(hi, (64, 128)), zero),
                    jnp.where(mask, jnp.broadcast_to(lo, (64, 128)), zero),
                ],
                0,
            )
        )
    parts = jnp.concatenate(parts, 1)
    return lax.dot_general(
        picks, parts, (((1,), (1,)), ((), ())), preferred_element_type=f32
    )


def wide(x):
    return jnp.concatenate([x[q : q + 1] for q in range(PER)], 1)


def narrow(x):
    return jnp.concatenate([x[:, q * LANES : (q + 1) * LANES] for q in range(PER)], 0)


def kernel(*refs):
    hbm = refs[:19]
    depth_out, east_out, south_out, river_out = refs[19:23]
    vm = refs[23:42]
    (
        level_send, level_here, link_channel, flow_send, flow_here,
        halo_up, halo_down, from_north, from_south,
        strip_east, strip_west, from_west, from_east, corners,
        old_send, old_before, carry_send, carry_all, shift_send, shift_all, weights,
        fields, levels, fixed, slope,
        in_sem, own_sem, send_sem, recv_sem, halo_send, halo_recv,
    ) = refs[42:]
    (
        water, bed, rough, wet, east, south, bank_row, bank_col, link_sec, link_reach,
        crest, factor, regime, channel, old, courant, junction, share, inflow,
    ) = vm

    gx, gy = lax.axis_index("gx"), lax.axis_index("gy")
    me = gx * NGY + gy
    z, core, y, x = gx // 2, lax.rem(gx, 2), gy // 4, lax.rem(gy, 4)

    order = [6, 7, 0, 1, 2, 3, 4, 5, 15, 16, 17, 14, 13, 8, 9, 10, 11, 12, 18]
    loads = {k: pltpu.make_async_copy(hbm[k], vm[k], in_sem.at[k]) for k in range(19)}
    for k in order:
        loads[k].start()

    zs = [lax.rem(z + d, 4) for d in range(4)]
    cs = [lax.rem(core + d, 2) for d in range(2)]
    ys = [lax.rem(y + d, 4) for d in range(4)]
    xs = [lax.rem(x + d, 4) for d in range(4)]
    peers = []
    for dz, dc, dy, dx in STEPS:
        px, py = zs[dz] * 2 + cs[dc], ys[dy] * 4 + xs[dx]
        peers.append((px, py, px * NGY + py))
    barrier = pltpu.get_barrier_semaphore()
    for px, py, _ in peers:
        pl.semaphore_signal(barrier, inc=1, device_id=(px, py), device_id_type=MESH)

    def remote(src, dst, send, recv, where):
        return pltpu.make_async_remote_copy(
            src_ref=src, dst_ref=dst, send_sem=send, recv_sem=recv,
            device_id=where, device_id_type=MESH,
        )

    def to_all(src, dst, n, k, same):
        for px, py, p in peers:
            remote(
                src if same else src.at[pl.ds(p * n, n)],
                dst.at[pl.ds(me * n, n)], send_sem.at[k], recv_sem.at[k], (px, py),
            ).start()
        own = pltpu.make_async_copy(
            src if same else src.at[pl.ds(me * n, n)], dst.at[pl.ds(me * n, n)], own_sem.at[k]
        )
        own.start()

        def arrived():
            part = dst.at[pl.ds(0, (DEV - 1) * n)]
            pltpu.make_async_copy(part, part, recv_sem.at[k]).wait()
            own.wait()

        def sent():
            part = dst.at[pl.ds(0, (DEV - 1) * n)]
            pltpu.make_async_copy(part, part, send_sem.at[k]).wait()

        return arrived, sent

    for k in (6, 7, 0, 1):
        loads[k].wait()
    level_table = jnp.concatenate(split2(bed[...] + water[...]), 0)

    def bank_cells(i):
        base = pl.multiple_of(i * G, G)
        at = [pl.ds(base + j, 1) for j in range(G)]
        return base, [bank_row[a, :] for a in at], [bank_col[a, :] for a in at]

    def gather_bank(i, c):
        base, rows, cols = bank_cells(i)
        level_send[pl.ds(base, G), :] = jnp.concatenate(
            gather_chunk(level_table, rows, cols), 0
        )
        return c

    lax.fori_loop(0, ROWS // G, gather_bank, 0)

    for k in (2, 3, 4, 5, 14):
        loads[k].wait()
    planes = (water, east, south, bed, rough, wet)
    lane = lax.broadcasted_iota(i32, (CX, 128), 1)
    pack_east = jnp.zeros((CX, 128), f32)
    pack_west = jnp.zeros((CX, 128), f32)
    for f, ref in enumerate(planes):
        halo_up[f] = ref[0:8, :].astype(f32)
        halo_down[f] = ref[CX - 8 : CX, :].astype(f32)
        right, left = ref[:, CY - 128 :].astype(f32), ref[:, :128].astype(f32)
        mine = (lane >= STRIP * f) & (lane < STRIP * f + 4)
        right = pltpu.roll(right, (STRIP * f + 4) % 128, 1)
        left = pltpu.roll(left, STRIP * f, 1) if f else left
        pack_east = jnp.where(mine, right, pack_east)
        pack_west = jnp.where(mine, left, pack_west)
    strip_east[...] = pack_east
    strip_west[...] = pack_west
    old_send[...] = old[SEC - 1 : SEC, :]

    pl.semaphore_wait(barrier, DEV - 1)

    level_arrived, level_sent = to_all(level_send, level_here, 2, 0, False)

    north, south_to = lax.rem(gx + NGX - 1, NGX), lax.rem(gx + 1, NGX)
    west, east_to = lax.rem(gy + NGY - 1, NGY), lax.rem(gy + 1, NGY)
    after = lax.rem(me + 1, DEV)
    top, bottom = pl.ds(0, 8), pl.ds(CX - 8, 8)
    halos = [
        (halo_up, from_south, (north, gy)),
        (halo_down, from_north, (south_to, gy)),
        (strip_east, from_west, (gx, east_to)),
        (strip_west, from_east, (gx, west)),
        (strip_east.at[top], corners.at[0], (north, east_to)),
        (strip_east.at[bottom], corners.at[1], (south_to, east_to)),
        (strip_west.at[top], corners.at[2], (north, west)),
        (strip_west.at[bottom], corners.at[3], (south_to, west)),
        (old_send, old_before, (after // NGY, lax.rem(after, NGY))),
    ]
    halos = [
        remote(src, dst, halo_send.at[k], halo_recv.at[k], where)
        for k, (src, dst, where) in enumerate(halos)
    ]
    for copy in halos:
        copy.start()

    for k in (15, 16, 17):
        loads[k].wait()
    sub = lax.broadcasted_iota(i32, (SEC, RIV), 0)
    cour = courant[...]
    inverse = 1.0 / (0.5 + IMPLICIT_WEIGHT * cour)
    passing = jnp.where(junction[...] == 1, share[...], 1.0)
    carry = passing * (IMPLICIT_WEIGHT * cour - 0.5) * inverse
    old_weight = passing * (0.5 + (1.0 - IMPLICIT_WEIGHT) * cour) * inverse
    slope[...] = LATERAL_SCALE * cour * inverse
    fixed[...] = (0.5 - (1.0 - IMPLICIT_WEIGHT) * cour) * inverse * old[...]
    levels[5] = old_weight
    for n in range(5):
        levels[n] = carry
        carry = jnp.where(sub >= (1 << n), carry * pltpu.roll(carry, 1 << n, 0), carry)
    levels[6] = carry
    carry_send[...] = narrow(carry[SEC - 1 :])

    for k in (13, 8, 9):
        loads[k].wait()
    channel_table = jnp.concatenate(
        split2(jnp.concatenate([channel[:, :CY], channel[:, CY:]], 0)), 0
    )

    def link_cells(i):
        base = pl.multiple_of(i * G, G)
        reach = [link_reach[pl.ds(base + j, 1), :] for j in range(G)]
        rows = [link_sec[pl.ds(base + j, 1), :] + ((q >> 8) << 5) for j, q in enumerate(reach)]
        return base, rows, [q & 255 for q in reach]

    def gather_channel(i, c):
        base, rows, cols = link_cells(i)
        link_channel[pl.ds(base, G), :] = jnp.concatenate(
            gather_chunk(channel_table, rows, cols), 0
        )
        return c

    lax.fori_loop(0, ROWS // G, gather_channel, 0)
    carry_arrived, carry_sent = to_all(carry_send, carry_all, PER, 1, True)

    for copy in halos:
        copy.wait_recv()
    sub8 = lax.broadcasted_iota(i32, (8, CY), 0)
    held = []
    lanes = lax.broadcasted_iota(i32, (PX, 128), 1)
    side = lax.broadcasted_iota(i32, (PX, 128), 0)
    low, high = gx < NGX - 1, gx > 0
    edge8 = lax.broadcasted_iota(i32, (8, 128), 0)
    rows_in = (side < CX) | ((side < CX + 4) & low) | ((side >= CX + 4) & high)
    strip_left = jnp.concatenate(
        [from_west[...], jnp.where(edge8 < 4, corners[0], corners[1])], 0
    )
    strip_right = jnp.concatenate(
        [from_east[...], jnp.where(edge8 < 4, corners[2], corners[3])], 0
    )
    strip_left = jnp.where(rows_in & (gy > 0), strip_left, 0.0)
    strip_right = jnp.where(rows_in & (gy < NGY - 1), strip_right, 0.0)
    for f, ref in enumerate(planes):
        beyond = jnp.where(
            sub8 < 4, jnp.where(low, from_south[f], 0.0), jnp.where(high, from_north[f], 0.0)
        )
        fields[f, 0:CX, 0:CY] = ref[...].astype(f32)
        fields[f, CX:PX, 0:CY] = beyond
        right = pltpu.roll(strip_right, (128 - STRIP * f) % 128, 1) if f else strip_right
        left = pltpu.roll(strip_left, (128 - STRIP * f - 4) % 128, 1)
        fields[f, :, CY:PY] = jnp.where(
            lanes < 4, right, jnp.where(lanes >= 124, left, 0.0)
        )
        held.append(fields[f])
    depth, q_east, q_south, ground, manning, wetness = held

    def of_east(a):
        return pltpu.roll(a, PY - 1, 1)

    def of_south(a):
        return pltpu.roll(a, PX - 1, 0)

    faces = []
    for move in (of_east, of_south):
        mean = 0.5 * (manning + move(manning))
        faces.append(
            (
                move,
                jnp.maximum(ground, move(ground)),
                GRAVITY * TIME_STEP * mean * mean,
                wetness * move(wetness),
            )
        )
    flux = [q_east, q_south]
    for _ in range(SUBSTEPS):
        surface = ground + depth
        for n, (move, top, rub, open_) in enumerate(faces):
            beside = move(surface)
            flow_depth = jnp.maximum(jnp.maximum(surface, beside) - top, MIN_FLOW_DEPTH)
            drive = flux[n] - (GRAVITY * TIME_STEP / SPACING) * flow_depth * (beside - surface)
            friction = 1.0 + rub * jnp.abs(flux[n]) * jnp.exp((-7.0 / 3.0) * jnp.log(flow_depth))
            flux[n] = open_ * drive / friction
        depth = depth + (TIME_STEP / SPACING) * (
            pltpu.roll(flux[0], 1, 1) - flux[0] + pltpu.roll(flux[1], 1, 0) - flux[1]
        )
    east_out[...] = flux[0][:CX, :CY]
    south_out[...] = flux[1][:CX, :CY]
    fields[0] = depth

    loads[18].wait()
    previous = jnp.where(
        sub == 0,
        jnp.where(me == 0, inflow[...], old_before[...]),
        pltpu.roll(old[...], 1, 0),
    )
    fixed[...] = fixed[...] + levels[5] * previous

    for k in (10, 11, 12):
        loads[k].wait()
    level_arrived()

    def flow_part(i, c):
        at = pl.ds(pl.multiple_of(i * 32, 32), 32)
        plain, chan, top, rule = level_here[at, :], link_channel[at, :], crest[at, :], regime[at, :]
        upper = jnp.maximum(chan - top, 0.0)
        lower = jnp.maximum(plain - top, 0.0)
        free = upper * jnp.sqrt(upper) - lower * jnp.sqrt(lower)
        drop = chan - plain
        drowned = drop * jnp.sqrt(jnp.abs(drop))
        flow_send[at, :] = factor[at, :] * jnp.where(
            rule == 1, free, jnp.where(rule == 2, drowned, 0.0)
        )
        return c

    lax.fori_loop(0, 8, flow_part, 0)
    flow_arrived, flow_sent = to_all(flow_send, flow_here, 2, 2, False)

    def scatter_lateral(i, acc):
        base, rows, cols = link_cells(i)
        return acc + scatter_chunk(
            [flow_send[pl.ds(base + j, 1), :] for j in range(G)], rows, cols
        )

    acc = lax.fori_loop(0, ROWS // G, scatter_lateral, jnp.zeros((CY, 128), f32)).T
    acc = acc[:64] + acc[64:]
    lateral = jnp.concatenate([acc[:SEC], acc[SEC:]], 1)

    shift = fixed[...] - slope[...] * lateral
    for n in range(5):
        shift = jnp.where(
            sub >= (1 << n), levels[n] * pltpu.roll(shift, 1 << n, 0) + shift, shift
        )
    fixed[...] = shift
    shift_send[...] = narrow(shift[SEC - 1 :])
    shift_arrived, shift_sent = to_all(shift_send, shift_all, PER, 3, True)

    carry_arrived()
    half = lax.broadcasted_iota(i32, (8, LANES), 0)
    run = jnp.ones((8, LANES), f32)
    for k in range(DEV // 2 - 1, -1, -1):
        upstream = (half // PER + 2 * k) < me
        both = jnp.where(upstream, carry_all[8 * k : 8 * k + 8, :], 1.0)
        swapped = pltpu.roll(both, 4, 0)
        weight = jnp.where(half < PER, swapped, 1.0) * run
        weights[8 * k : 8 * k + 8, :] = jnp.where(upstream, weight, 0.0)
        run = run * (both * swapped)
    start = wide(run[:PER]) * inflow[...]

    flow_arrived()

    def scatter_bank(i, acc):
        base, rows, cols = bank_cells(i)
        return acc + scatter_chunk(
            [flow_here[pl.ds(base + j, 1), :] for j in range(G)], rows, cols
        )

    acc = lax.fori_loop(0, ROWS // G, scatter_bank, jnp.zeros((CY, 128), f32)).T
    depth_out[...] = fields[0, 0:CX, 0:CY] + BANK_GAIN * (acc[:64] + acc[64:])

    shift_arrived()
    parts = [
        weights[8 * k : 8 * k + 8, :] * shift_all[8 * k : 8 * k + 8, :] for k in range(DEV // 2)
    ]
    while len(parts) > 1:
        parts = [u + v for u, v in zip(parts[::2], parts[1::2])]
    enters = start + wide(parts[0][:PER] + parts[0][PER:])
    river_out[...] = levels[6] * enters + fixed[...]

    for sent in (level_sent, carry_sent, flow_sent, shift_sent):
        sent()
    for copy in halos:
        copy.wait_send()


def on_device(*args):
    args = list(args)
    for k in range(6, 13):
        args[k] = args[k].reshape(ROWS, 128)
    args[18] = args[18].reshape(1, RIV)
    vmem = lambda *shape: pltpu.VMEM(shape, f32)
    dma = pltpu.SemaphoreType.DMA
    scratch = [pltpu.VMEM(a.shape, a.dtype) for a in args]
    scratch += [vmem(ROWS, 128)] * 5
    scratch += [vmem(6, 8, CY)] * 4
    scratch += [vmem(CX, 128)] * 4 + [vmem(4, 8, 128)]
    scratch += [vmem(1, RIV)] * 2
    scratch += [vmem(PER, LANES), vmem(DEV * PER, LANES)] * 2 + [vmem(DEV * PER, LANES)]
    scratch += [vmem(6, PX, PY), vmem(7, SEC, RIV), vmem(SEC, RIV), vmem(SEC, RIV)]
    scratch += [dma((19,)), dma((4,)), dma((4,)), dma((4,)), dma((9,)), dma((9,))]
    return pl.pallas_call(
        kernel,
        out_shape=(
            jax.ShapeDtypeStruct((CX, CY), f32),
            jax.ShapeDtypeStruct((CX, CY), f32),
            jax.ShapeDtypeStruct((CX, CY), f32),
            jax.ShapeDtypeStruct((SEC, RIV), f32),
        ),
        in_specs=[pl.BlockSpec(memory_space=pl.ANY)] * 19,
        out_specs=[pl.BlockSpec(memory_space=pltpu.VMEM)] * 4,
        scratch_shapes=scratch,
        compiler_params=pltpu.CompilerParams(
            collective_id=0, has_side_effects=True, vmem_limit_bytes=62 << 20
        ),
        cost_estimate=pl.CostEstimate(
            flops=8 * 10**9, bytes_accessed=2 * 10**6, transcendentals=10**6
        ),
        name="coupled_step",
    )(*args)


def solution(mesh):
    tile, flat, chain = P("gx", "gy"), P(("gx", "gy")), P(("gx", "gy"), None)
    in_specs = (tile,) * 6 + (flat,) * 7 + (chain,) * 5 + (P(),)
    out_specs = (tile, tile, tile, chain)
    return jax.shard_map(
        on_device, mesh=mesh, in_specs=in_specs, out_specs=out_specs, check_vma=False
    )
```

time: 58.3 us -> 35.9 us (0.62); the launches traced: 57.5 us -> 35.7 us
  local copies, waits for them, and re-layouts: 18.7 us -> 3.86 us
  Pallas kernels: 38.1 us -> 31.2 us
    unnamed x42 -> x10, local copies, waits for them, and re-layouts: 18.7 us -> 3.86 us
    pallas_call x1, Pallas kernels: 38.1 us -> 31.2 us  [on_device(): pl.pallas_call(kernel, out_shape=(jax.ShapeDtypeStruct((CX, CY), f32), ja...]
where the time goes in v2:
time: 35.9 us; the launch traced here: 35.7 us
  Pallas kernels  31.2 us (87%)
  local copies, waits for them, and re-layouts  3.86 us (11%)
  between operations  0.66 us (2%)
    pallas_call x1, Pallas kernels, on_device(): pl.pallas_call(kernel, out_shape=(jax.ShapeDtypeStruct((CX, CY), f32), ja...  31.2 us
    unnamed x10, local copies, waits for them, and re-layouts  3.86 us

profile of v2, /device:TPU:1, one launch (start us, length us, event | category | flops | bytes accessed | tf_op | source)
XLA Modules:
  0.0 35.7 jit_solution(4511772090092561645)
XLA Ops:
  0.6 31.2 %coupled_step.1 = (f32[64,256]{1,0:T(8,128)}, f32[64,256]{1,0:T(8,128)}, f32[64,256]{1,0:T(8,128)}, f32[32,512]{1,0:T(8,128)}) custom-call(f32[64,256]{1,0:T(8,128)} %refs_0_.1, f32[64,256]{1,0:T(8,128)} %refs_1_.1, f32[64,256]{1,0:T(8,128)} %refs_2_.1, s32[64,256]{1,0:T(8,128)} %refs_3_.1, f32[64,256]{1,0:T(8,128)} %refs_4_.1, f32[64,256]{1,0:T(8,128)} %refs_5_.1, ...), custom_call_target="tpu_custom_call" | custom-call | flops 8000000000 | bytes 2000000 | tf_op jit(solution)/shard_map/coupled_step/pallas_call | solution.py:431
  31.8 0.0 copy-start.2
  31.8 1.5 %copy.27 = f32[64,256]{1,0:T(8,128)} copy(f32[64,256]{1,0:T(8,128)} %get-tuple-element.8) | data formatting | bytes 131072
  33.3 0.0 copy-done.2
  33.3 0.0 copy-start.1
  33.3 0.6 %copy.28 = f32[64,256]{1,0:T(8,128)} copy(f32[64,256]{1,0:T(8,128)S(1)} %copy-done.2) | data formatting | bytes 131072
  34.0 0.2 copy-done.1
  34.2 0.0 copy-start
  34.2 0.6 %copy.29 = f32[64,256]{1,0:T(8,128)} copy(f32[64,256]{1,0:T(8,128)S(1)} %copy-done.1) | data formatting | bytes 131072
  34.8 0.2 copy-done
  35.1 0.6 %copy.30 = f32[32,512]{1,0:T(8,128)} copy(f32[32,512]{1,0:T(8,128)S(1)} %copy-done) | data formatting | bytes 131072
Async XLA Ops:
  31.8 1.5 %copy-start.2 = (f32[64,256]{1,0:T(8,128)S(1)}, f32[64,256]{1,0:T(8,128)}, u32[]{:S(2)}) copy-start(f32[64,256]{1,0:T(8,128)} %get-tuple-element.9) | copy-start | bytes 196612
  33.3 0.9 %copy-start.1 = (f32[64,256]{1,0:T(8,128)S(1)}, f32[64,256]{1,0:T(8,128)}, u32[]{:S(2)}) copy-start(f32[64,256]{1,0:T(8,128)} %get-tuple-element.10) | copy-start | bytes 196612
  34.2 0.9 %copy-start = (f32[32,512]{1,0:T(8,128)S(1)}, f32[32,512]{1,0:T(8,128)}, u32[]{:S(2)}) copy-start(f32[32,512]{1,0:T(8,128)} %get-tuple-element.11) | copy-start | bytes 196612

commit v3 on v2

--- a/solution.py
+++ b/solution.py
@@ -413,6 +413,14 @@
         copy.wait_send()
 
 
+def write_out(*refs):
+    copies = [pltpu.make_async_copy(refs[k], refs[4 + k], refs[8].at[k]) for k in range(4)]
+    for copy in copies:
+        copy.start()
+    for copy in copies:
+        copy.wait()
+
+
 def on_device(*args):
     args = list(args)
     for k in range(6, 13):
@@ -428,14 +436,9 @@
     scratch += [vmem(PER, LANES), vmem(DEV * PER, LANES)] * 2 + [vmem(DEV * PER, LANES)]
     scratch += [vmem(6, PX, PY), vmem(7, SEC, RIV), vmem(SEC, RIV), vmem(SEC, RIV)]
     scratch += [dma((19,)), dma((4,)), dma((4,)), dma((4,)), dma((9,)), dma((9,))]
-    return pl.pallas_call(
+    results = pl.pallas_call(
         kernel,
-        out_shape=(
-            jax.ShapeDtypeStruct((CX, CY), f32),
-            jax.ShapeDtypeStruct((CX, CY), f32),
-            jax.ShapeDtypeStruct((CX, CY), f32),
-            jax.ShapeDtypeStruct((SEC, RIV), f32),
-        ),
+        out_shape=(vmem(CX, CY), vmem(CX, CY), vmem(CX, CY), vmem(SEC, RIV)),
         in_specs=[pl.BlockSpec(memory_space=pl.ANY)] * 19,
         out_specs=[pl.BlockSpec(memory_space=pltpu.VMEM)] * 4,
         scratch_shapes=scratch,
@@ -447,6 +450,14 @@
         ),
         name="coupled_step",
     )(*args)
+    return pl.pallas_call(
+        write_out,
+        out_shape=[jax.ShapeDtypeStruct(r.shape, f32) for r in results],
+        in_specs=[pl.BlockSpec(memory_space=pltpu.VMEM)] * 4,
+        out_specs=[pl.BlockSpec(memory_space=pl.ANY)] * 4,
+        scratch_shapes=[dma((4,))],
+        name="write_out",
+    )(*[pltpu.with_memory_space_constraint(r, pltpu.VMEM) for r in results])
 
 
 def solution(mesh):

time: 35.9 us -> 32 us (0.89)
  local copies, waits for them, and re-layouts: 3.86 us -> 0 us
    unnamed x10 -> x0, local copies, waits for them, and re-layouts: 3.86 us -> none
    pallas_call x1 -> x2, Pallas kernels: 31.2 us -> 31.2 us  [the longest x1 30.5 us: on_device(): pl.pallas_call(kernel, out_shape=(vmem(CX, CY), vmem(CX, CY), vmem(CX, CY...]
where the time goes in v3:
time: 32 us; the launch traced here: 31.9 us
  Pallas kernels  31.2 us (98%)
  between operations  0.65 us (2%)
    pallas_call x1, Pallas kernels, on_device(): pl.pallas_call(kernel, out_shape=(vmem(CX, CY), vmem(CX, CY), vmem(CX, CY...  30.5 us
    pallas_call x1, Pallas kernels, on_device(): pl.pallas_call(write_out, out_shape=[jax.ShapeDtypeStruct(r.shape, f32) f...  0.73 us

profile of v3, /device:TPU:1, one launch (start us, length us, event | category | flops | bytes accessed | tf_op | source)
XLA Modules:
  0.0 31.9 jit_solution(18031366684554934020)
XLA Ops:
  0.6 30.5 %coupled_step.1 = (f32[64,256]{1,0:T(8,128)S(1)}, f32[64,256]{1,0:T(8,128)S(1)}, f32[64,256]{1,0:T(8,128)S(1)}, f32[32,512]{1,0:T(8,128)S(1)}) custom-call(f32[64,256]{1,0:T(8,128)} %refs_0_.1, f32[64,256]{1,0:T(8,128)} %refs_1_.1, f32[64,256]{1,0:T(8,128)} %refs_2_.1, s32[64,256]{1,0:T(8,128)} %refs_3_.1, f32[64,256]{1,0:T(8,128)} %refs_4_.1, ...), custom_call_target="tpu_custom_call" | custom-call | flops 8000000000 | bytes 2000000 | tf_op jit(solution)/shard_map/coupled_step/pallas_call | solution.py:439
  31.1 0.7 %write_out.1 = (f32[64,256]{1,0:T(8,128)}, f32[64,256]{1,0:T(8,128)}, f32[64,256]{1,0:T(8,128)}, f32[32,512]{1,0:T(8,128)}) custom-call(f32[64,256]{1,0:T(8,128)S(1)} %get-tuple-element.8.refs_0_, f32[64,256]{1,0:T(8,128)S(1)} %get-tuple-element.9.refs_1_, f32[64,256]{1,0:T(8,128)S(1)} %get-tuple-element.10.refs_2_, f32[32,512]{1,0:T(8,128)S(1)} %get-tuple-element.11.refs_3_), custom_call_target="tpu_custom_call" | custom-call | tf_op jit(solution)/shard_map/write_out/pallas_call | solution.py:453

commit v4 on v3

--- a/solution.py
+++ b/solution.py
@@ -119,7 +119,8 @@
 
     order = [6, 7, 0, 1, 2, 3, 4, 5, 15, 16, 17, 14, 13, 8, 9, 10, 11, 12, 18]
     loads = {k: pltpu.make_async_copy(hbm[k], vm[k], in_sem.at[k]) for k in range(19)}
-    for k in order:
+
+    for k in order[:4]:
         loads[k].start()
 
     zs = [lax.rem(z + d, 4) for d in range(4)]
@@ -133,6 +134,8 @@
     barrier = pltpu.get_barrier_semaphore()
     for px, py, _ in peers:
         pl.semaphore_signal(barrier, inc=1, device_id=(px, py), device_id_type=MESH)
+    for k in order[4:]:
+        loads[k].start()
 
     def remote(src, dst, send, recv, where):
         return pltpu.make_async_remote_copy(
@@ -264,7 +267,55 @@
     lax.fori_loop(0, ROWS // G, gather_channel, 0)
     carry_arrived, carry_sent = to_all(carry_send, carry_all, PER, 1, True)
 
-    for copy in halos:
+    halos[8].wait_recv()
+    loads[18].wait()
+    previous = jnp.where(
+        sub == 0,
+        jnp.where(me == 0, inflow[...], old_before[...]),
+        pltpu.roll(old[...], 1, 0),
+    )
+    fixed[...] = fixed[...] + levels[5] * previous
+
+    for k in (10, 11, 12):
+        loads[k].wait()
+    level_arrived()
+
+    def flow_part(i, c):
+        at = pl.ds(pl.multiple_of(i * 32, 32), 32)
+        plain, chan, top, rule = level_here[at, :], link_channel[at, :], crest[at, :], regime[at, :]
+        upper = jnp.maximum(chan - top, 0.0)
+        lower = jnp.maximum(plain - top, 0.0)
+        free = upper * jnp.sqrt(upper) - lower * jnp.sqrt(lower)
+        drop = chan - plain
+        drowned = drop * jnp.sqrt(jnp.abs(drop))
+        flow_send[at, :] = factor[at, :] * jnp.where(
+            rule == 1, free, jnp.where(rule == 2, drowned, 0.0)
+        )
+        return c
+
+    lax.fori_loop(0, 8, flow_part, 0)
+    flow_arrived, flow_sent = to_all(flow_send, flow_here, 2, 2, False)
+
+    def scatter_lateral(i, acc):
+        base, rows, cols = link_cells(i)
+        return acc + scatter_chunk(
+            [flow_send[pl.ds(base + j, 1), :] for j in range(G)], rows, cols
+        )
+
+    acc = lax.fori_loop(0, ROWS // G, scatter_lateral, jnp.zeros((CY, 128), f32)).T
+    acc = acc[:64] + acc[64:]
+    lateral = jnp.concatenate([acc[:SEC], acc[SEC:]], 1)
+
+    shift = fixed[...] - slope[...] * lateral
+    for n in range(5):
+        shift = jnp.where(
+            sub >= (1 << n), levels[n] * pltpu.roll(shift, 1 << n, 0) + shift, shift
+        )
+    fixed[...] = shift
+    shift_send[...] = narrow(shift[SEC - 1 :])
+    shift_arrived, shift_sent = to_all(shift_send, shift_all, PER, 3, True)
+
+    for copy in halos[:8]:
         copy.wait_recv()
     sub8 = lax.broadcasted_iota(i32, (8, CY), 0)
     held = []
@@ -327,53 +378,6 @@
     east_out[...] = flux[0][:CX, :CY]
     south_out[...] = flux[1][:CX, :CY]
     fields[0] = depth
-
-    loads[18].wait()
-    previous = jnp.where(
-        sub == 0,
-        jnp.where(me == 0, inflow[...], old_before[...]),
-        pltpu.roll(old[...], 1, 0),
-    )
-    fixed[...] = fixed[...] + levels[5] * previous
-
-    for k in (10, 11, 12):
-        loads[k].wait()
-    level_arrived()
-
-    def flow_part(i, c):
-        at = pl.ds(pl.multiple_of(i * 32, 32), 32)
-        plain, chan, top, rule = level_here[at, :], link_channel[at, :], crest[at, :], regime[at, :]
-        upper = jnp.maximum(chan - top, 0.0)
-        lower = jnp.maximum(plain - top, 0.0)
-        free = upper * jnp.sqrt(upper) - lower * jnp.sqrt(lower)
-        drop = chan - plain
-        drowned = drop * jnp.sqrt(jnp.abs(drop))
-        flow_send[at, :] = factor[at, :] * jnp.where(
-            rule == 1, free, jnp.where(rule == 2, drowned, 0.0)
-        )
-        return c
-
-    lax.fori_loop(0, 8, flow_part, 0)
-    flow_arrived, flow_sent = to_all(flow_send, flow_here, 2, 2, False)
-
-    def scatter_lateral(i, acc):
-        base, rows, cols = link_cells(i)
-        return acc + scatter_chunk(
-            [flow_send[pl.ds(base + j, 1), :] for j in range(G)], rows, cols
-        )
-
-    acc = lax.fori_loop(0, ROWS // G, scatter_lateral, jnp.zeros((CY, 128), f32)).T
-    acc = acc[:64] + acc[64:]
-    lateral = jnp.concatenate([acc[:SEC], acc[SEC:]], 1)
-
-    shift = fixed[...] - slope[...] * lateral
-    for n in range(5):
-        shift = jnp.where(
-            sub >= (1 << n), levels[n] * pltpu.roll(shift, 1 << n, 0) + shift, shift
-        )
-    fixed[...] = shift
-    shift_send[...] = narrow(shift[SEC - 1 :])
-    shift_arrived, shift_sent = to_all(shift_send, shift_all, PER, 3, True)
 
     carry_arrived()
     half = lax.broadcasted_iota(i32, (8, LANES), 0)

time: 32 us -> 31 us (0.969)
  Pallas kernels: 31.2 us -> 30.3 us
    pallas_call x1, Pallas kernels: 30.5 us -> 29.5 us  [on_device(): pl.pallas_call(kernel, out_shape=(vmem(CX, CY), vmem(CX, CY), vmem(CX, CY...]
where the time goes in v4:
time: 31 us; the launch traced here: 30.9 us
  Pallas kernels  30.3 us (98%)
  between operations  0.65 us (2%)
    pallas_call x1, Pallas kernels, on_device(): pl.pallas_call(kernel, out_shape=(vmem(CX, CY), vmem(CX, CY), vmem(CX, CY...  29.5 us
    pallas_call x1, Pallas kernels, on_device(): pl.pallas_call(write_out, out_shape=[jax.ShapeDtypeStruct(r.shape, f32) f...  0.73 us

profile of v4, /device:TPU:1, one launch (start us, length us, event | category | flops | bytes accessed | tf_op | source)
XLA Modules:
  0.0 30.9 jit_solution(13819353602066981104)
XLA Ops:
  0.6 29.5 %coupled_step.1 = (f32[64,256]{1,0:T(8,128)S(1)}, f32[64,256]{1,0:T(8,128)S(1)}, f32[64,256]{1,0:T(8,128)S(1)}, f32[32,512]{1,0:T(8,128)S(1)}) custom-call(f32[64,256]{1,0:T(8,128)} %refs_0_.1, f32[64,256]{1,0:T(8,128)} %refs_1_.1, f32[64,256]{1,0:T(8,128)} %refs_2_.1, s32[64,256]{1,0:T(8,128)} %refs_3_.1, f32[64,256]{1,0:T(8,128)} %refs_4_.1, ...), custom_call_target="tpu_custom_call" | custom-call | flops 8000000000 | bytes 2000000 | tf_op jit(solution)/shard_map/coupled_step/pallas_call | solution.py:443
  30.2 0.7 %write_out.1 = (f32[64,256]{1,0:T(8,128)}, f32[64,256]{1,0:T(8,128)}, f32[64,256]{1,0:T(8,128)}, f32[32,512]{1,0:T(8,128)}) custom-call(f32[64,256]{1,0:T(8,128)S(1)} %get-tuple-element.8.refs_0_, f32[64,256]{1,0:T(8,128)S(1)} %get-tuple-element.9.refs_1_, f32[64,256]{1,0:T(8,128)S(1)} %get-tuple-element.10.refs_2_, f32[32,512]{1,0:T(8,128)S(1)} %get-tuple-element.11.refs_3_), custom_call_target="tpu_custom_call" | custom-call | tf_op jit(solution)/shard_map/write_out/pallas_call | solution.py:457

commit v5 on v4

--- a/solution.py
+++ b/solution.py
@@ -53,9 +53,9 @@
     return jnp.where(iota == index, jnp.ones((), bf16), jnp.zeros((), bf16))
 
 
-def gather_chunk(table, rows, cols):
+def gather_chunk(table, rows, picks):
     iota = lax.broadcasted_iota(i32, (64, 128), 0)
-    picks = jnp.concatenate([one_hot(c, 256) for c in cols], 1)
+    picks = jnp.concatenate(picks, 1)
     both = jnp.dot(table, picks, preferred_element_type=f32)
     both = both[:64] + both[64:]
     out = []
@@ -65,26 +65,24 @@
     return out
 
 
-def scatter_chunk(flows, rows, cols):
+def row_parts(flows, rows):
     iota = lax.broadcasted_iota(i16, (64, 128), 0)
     zero = jnp.zeros((), bf16)
-    picks = jnp.concatenate([one_hot(c, 256) for c in cols], 1)
     parts = []
     for flow, r in zip(flows, rows):
-        hi, lo = split2(flow)
         mask = iota == jnp.broadcast_to(r.astype(i16), (64, 128))
         parts.append(
             jnp.concatenate(
-                [
-                    jnp.where(mask, jnp.broadcast_to(hi, (64, 128)), zero),
-                    jnp.where(mask, jnp.broadcast_to(lo, (64, 128)), zero),
-                ],
-                0,
+                [jnp.where(mask, jnp.broadcast_to(p, (64, 128)), zero) for p in split2(flow)], 0
             )
         )
-    parts = jnp.concatenate(parts, 1)
+    return jnp.concatenate(parts, 1)
+
+
+def scatter_chunk(flows, rows, cols):
+    picks = jnp.concatenate([one_hot(c, 256) for c in cols], 1)
     return lax.dot_general(
-        picks, parts, (((1,), (1,)), ((), ())), preferred_element_type=f32
+        picks, row_parts(flows, rows), (((1,), (1,)), ((), ())), preferred_element_type=f32
     )
 
 
@@ -105,7 +103,7 @@
         halo_up, halo_down, from_north, from_south,
         strip_east, strip_west, from_west, from_east, corners,
         old_send, old_before, carry_send, carry_all, shift_send, shift_all, weights,
-        fields, levels, fixed, slope,
+        fields, levels, fixed, slope, link_picks,
         in_sem, own_sem, send_sem, recv_sem, halo_send, halo_recv,
     ) = refs[42:]
     (
@@ -177,7 +175,7 @@
     def gather_bank(i, c):
         base, rows, cols = bank_cells(i)
         level_send[pl.ds(base, G), :] = jnp.concatenate(
-            gather_chunk(level_table, rows, cols), 0
+            gather_chunk(level_table, rows, [one_hot(q, CY) for q in cols]), 0
         )
         return c
 
@@ -259,13 +257,31 @@
 
     def gather_channel(i, c):
         base, rows, cols = link_cells(i)
+        picks = [one_hot(q, CY) for q in cols]
+        for j, pick in enumerate(picks):
+            link_picks[pl.ds(pl.multiple_of((base + j) * LANES, LANES), LANES), :] = pick.T
         link_channel[pl.ds(base, G), :] = jnp.concatenate(
-            gather_chunk(channel_table, rows, cols), 0
+            gather_chunk(channel_table, rows, picks), 0
         )
         return c
 
     lax.fori_loop(0, ROWS // G, gather_channel, 0)
-    carry_arrived, carry_sent = to_all(carry_send, carry_all, PER, 1, True)
+
+    own_carry = pltpu.make_async_copy(
+        carry_send, carry_all.at[pl.ds(me * PER, PER)], own_sem.at[1]
+    )
+    own_carry.start()
+    for dz, dc, dy, dx in STEPS:
+        if dz == 0 and dc == 0:
+            remote(
+                carry_send, carry_all.at[pl.ds(me * PER, PER)], send_sem.at[1], recv_sem.at[1],
+                (gx, ys[dy] * 4 + xs[dx]),
+            ).start()
+
+    def drain(rows, sem):
+        part = carry_all.at[pl.ds(0, rows)]
+        pltpu.make_async_copy(part, part, sem).wait()
+
 
     halos[8].wait_recv()
     loads[18].wait()
@@ -297,14 +313,23 @@
     flow_arrived, flow_sent = to_all(flow_send, flow_here, 2, 2, False)
 
     def scatter_lateral(i, acc):
-        base, rows, cols = link_cells(i)
-        return acc + scatter_chunk(
-            [flow_send[pl.ds(base + j, 1), :] for j in range(G)], rows, cols
-        )
-
-    acc = lax.fori_loop(0, ROWS // G, scatter_lateral, jnp.zeros((CY, 128), f32)).T
+        base, rows, _ = link_cells(i)
+        parts = row_parts([flow_send[pl.ds(base + j, 1), :] for j in range(G)], rows)
+        picks = link_picks[pl.ds(pl.multiple_of(base * LANES, LANES), G * LANES), :]
+        return acc + jnp.dot(parts, picks, preferred_element_type=f32)
+
+    acc = lax.fori_loop(0, ROWS // G, scatter_lateral, jnp.zeros((128, CY), f32))
     acc = acc[:64] + acc[64:]
     lateral = jnp.concatenate([acc[:SEC], acc[SEC:]], 1)
+
+    own_carry.wait()
+    drain((NGY - 1) * PER, recv_sem.at[1])
+    block = carry_all.at[pl.ds(gx * (NGY * PER), NGY * PER)]
+    for dz, dc, dy, dx in STEPS:
+        if dy == 0 and dx == 0:
+            remote(
+                block, block, send_sem.at[4], recv_sem.at[4], (zs[dz] * 2 + cs[dc], gy)
+            ).start()
 
     shift = fixed[...] - slope[...] * lateral
     for n in range(5):
@@ -379,7 +404,18 @@
     south_out[...] = flux[1][:CX, :CY]
     fields[0] = depth
 
-    carry_arrived()
+    flow_arrived()
+
+    def scatter_bank(i, acc):
+        base, rows, cols = bank_cells(i)
+        return acc + scatter_chunk(
+            [flow_here[pl.ds(base + j, 1), :] for j in range(G)], rows, cols
+        )
+
+    acc = lax.fori_loop(0, ROWS // G, scatter_bank, jnp.zeros((CY, 128), f32)).T
+    depth_out[...] = fields[0, 0:CX, 0:CY] + BANK_GAIN * (acc[:64] + acc[64:])
+
+    drain((NGX - 1) * NGY * PER, recv_sem.at[4])
     half = lax.broadcasted_iota(i32, (8, LANES), 0)
     run = jnp.ones((8, LANES), f32)
     for k in range(DEV // 2 - 1, -1, -1):
@@ -391,17 +427,6 @@
         run = run * (both * swapped)
     start = wide(run[:PER]) * inflow[...]
 
-    flow_arrived()
-
-    def scatter_bank(i, acc):
-        base, rows, cols = bank_cells(i)
-        return acc + scatter_chunk(
-            [flow_here[pl.ds(base + j, 1), :] for j in range(G)], rows, cols
-        )
-
-    acc = lax.fori_loop(0, ROWS // G, scatter_bank, jnp.zeros((CY, 128), f32)).T
-    depth_out[...] = fields[0, 0:CX, 0:CY] + BANK_GAIN * (acc[:64] + acc[64:])
-
     shift_arrived()
     parts = [
         weights[8 * k : 8 * k + 8, :] * shift_all[8 * k : 8 * k + 8, :] for k in range(DEV // 2)
@@ -411,8 +436,10 @@
     enters = start + wide(parts[0][:PER] + parts[0][PER:])
     river_out[...] = levels[6] * enters + fixed[...]
 
-    for sent in (level_sent, carry_sent, flow_sent, shift_sent):
+    for sent in (level_sent, flow_sent, shift_sent):
         sent()
+    drain((NGY - 1) * PER, send_sem.at[1])
+    drain((NGX - 1) * NGY * PER, send_sem.at[4])
     for copy in halos:
         copy.wait_send()
 
@@ -439,7 +466,8 @@
     scratch += [vmem(1, RIV)] * 2
     scratch += [vmem(PER, LANES), vmem(DEV * PER, LANES)] * 2 + [vmem(DEV * PER, LANES)]
     scratch += [vmem(6, PX, PY), vmem(7, SEC, RIV), vmem(SEC, RIV), vmem(SEC, RIV)]
-    scratch += [dma((19,)), dma((4,)), dma((4,)), dma((4,)), dma((9,)), dma((9,))]
+    scratch += [pltpu.VMEM((ROWS * LANES, CY), bf16)]
+    scratch += [dma((19,)), dma((4,)), dma((5,)), dma((5,)), dma((9,)), dma((9,))]
     results = pl.pallas_call(
         kernel,
         out_shape=(vmem(CX, CY), vmem(CX, CY), vmem(CX, CY), vmem(SEC, RIV)),

time: 31 us -> 30.4 us (0.981)
  Pallas kernels: 30.3 us -> 29.7 us
    pallas_call x1, Pallas kernels: 29.5 us -> 28.9 us  [on_device(): pl.pallas_call(kernel, out_shape=(vmem(CX, CY), vmem(CX, CY), vmem(CX, CY...]
where the time goes in v5:
time: 30.4 us; the launch traced here: 30.3 us
  Pallas kernels  29.7 us (98%)
  between operations  0.65 us (2%)
    pallas_call x1, Pallas kernels, on_device(): pl.pallas_call(kernel, out_shape=(vmem(CX, CY), vmem(CX, CY), vmem(CX, CY...  28.9 us
    pallas_call x1, Pallas kernels, on_device(): pl.pallas_call(write_out, out_shape=[jax.ShapeDtypeStruct(r.shape, f32) f...  0.73 us

profile of v5, /device:TPU:1, one launch (start us, length us, event | category | flops | bytes accessed | tf_op | source)
XLA Modules:
  0.0 30.3 jit_solution(4405049438721932072)
XLA Ops:
  0.6 28.9 %coupled_step.1 = (f32[64,256]{1,0:T(8,128)S(1)}, f32[64,256]{1,0:T(8,128)S(1)}, f32[64,256]{1,0:T(8,128)S(1)}, f32[32,512]{1,0:T(8,128)S(1)}) custom-call(f32[64,256]{1,0:T(8,128)} %refs_0_.1, f32[64,256]{1,0:T(8,128)} %refs_1_.1, f32[64,256]{1,0:T(8,128)} %refs_2_.1, s32[64,256]{1,0:T(8,128)} %refs_3_.1, f32[64,256]{1,0:T(8,128)} %refs_4_.1, ...), custom_call_target="tpu_custom_call" | custom-call | flops 8000000000 | bytes 2000000 | tf_op jit(solution)/shard_map/coupled_step/pallas_call | solution.py:471
  29.6 0.7 %write_out.1 = (f32[64,256]{1,0:T(8,128)}, f32[64,256]{1,0:T(8,128)}, f32[64,256]{1,0:T(8,128)}, f32[32,512]{1,0:T(8,128)}) custom-call(f32[64,256]{1,0:T(8,128)S(1)} %get-tuple-element.8.refs_0_, f32[64,256]{1,0:T(8,128)S(1)} %get-tuple-element.9.refs_1_, f32[64,256]{1,0:T(8,128)S(1)} %get-tuple-element.10.refs_2_, f32[32,512]{1,0:T(8,128)S(1)} %get-tuple-element.11.refs_3_), custom_call_target="tpu_custom_call" | custom-call | tf_op jit(solution)/shard_map/write_out/pallas_call | solution.py:485

commit v6 on v5

--- a/solution.py
+++ b/solution.py
@@ -180,6 +180,10 @@
         return c
 
     lax.fori_loop(0, ROWS // G, gather_bank, 0)
+
+    pl.semaphore_wait(barrier, DEV - 1)
+
+    level_arrived, level_sent = to_all(level_send, level_here, 2, 0, False)
 
     for k in (2, 3, 4, 5, 14):
         loads[k].wait()
@@ -200,9 +204,6 @@
     strip_west[...] = pack_west
     old_send[...] = old[SEC - 1 : SEC, :]
 
-    pl.semaphore_wait(barrier, DEV - 1)
-
-    level_arrived, level_sent = to_all(level_send, level_here, 2, 0, False)
 
     north, south_to = lax.rem(gx + NGX - 1, NGX), lax.rem(gx + 1, NGX)
     west, east_to = lax.rem(gy + NGY - 1, NGY), lax.rem(gy + 1, NGY)

time: 30.4 us -> 30.4 us (level)
  no operation moved by 1% of the time
where the time goes in v6:
time: 30.4 us; the launch traced here: 30.3 us
  Pallas kernels  29.7 us (98%)
  between operations  0.65 us (2%)
    pallas_call x1, Pallas kernels, on_device(): pl.pallas_call(kernel, out_shape=(vmem(CX, CY), vmem(CX, CY), vmem(CX, CY...  28.9 us
    pallas_call x1, Pallas kernels, on_device(): pl.pallas_call(write_out, out_shape=[jax.ShapeDtypeStruct(r.shape, f32) f...  0.73 us

profile of v6, /device:TPU:1, one launch (start us, length us, event | category | flops | bytes accessed | tf_op | source)
XLA Modules:
  0.0 30.3 jit_solution(9156807864115493965)
XLA Ops:
  0.6 28.9 %coupled_step.1 = (f32[64,256]{1,0:T(8,128)S(1)}, f32[64,256]{1,0:T(8,128)S(1)}, f32[64,256]{1,0:T(8,128)S(1)}, f32[32,512]{1,0:T(8,128)S(1)}) custom-call(f32[64,256]{1,0:T(8,128)} %refs_0_.1, f32[64,256]{1,0:T(8,128)} %refs_1_.1, f32[64,256]{1,0:T(8,128)} %refs_2_.1, s32[64,256]{1,0:T(8,128)} %refs_3_.1, f32[64,256]{1,0:T(8,128)} %refs_4_.1, ...), custom_call_target="tpu_custom_call" | custom-call | flops 8000000000 | bytes 2000000 | tf_op jit(solution)/shard_map/coupled_step/pallas_call | solution.py:472
  29.6 0.7 %write_out.1 = (f32[64,256]{1,0:T(8,128)}, f32[64,256]{1,0:T(8,128)}, f32[64,256]{1,0:T(8,128)}, f32[32,512]{1,0:T(8,128)}) custom-call(f32[64,256]{1,0:T(8,128)S(1)} %get-tuple-element.8.refs_0_, f32[64,256]{1,0:T(8,128)S(1)} %get-tuple-element.9.refs_1_, f32[64,256]{1,0:T(8,128)S(1)} %get-tuple-element.10.refs_2_, f32[32,512]{1,0:T(8,128)S(1)} %get-tuple-element.11.refs_3_), custom_call_target="tpu_custom_call" | custom-call | tf_op jit(solution)/shard_map/write_out/pallas_call | solution.py:486
